TPU v7x, 768 devices: a whole 4x8x12 slice. The times are simulated.
768 devices in a mesh: dp: 64 (over y, z_hi, x), seq: 12 (over z_lo, core).
Axes of the slice: x: 4, y: 8, z: 12 (z_hi: 2, z_lo: 6; z = z_hi * 6 + z_lo), core: 2. Of those that a mesh axis runs over, the one named last changes fastest.
Arguments:
- tiles: bfloat16 [64, 24, 64, 588], P('dp', 'seq'), may hold values from -6 to 6
- tile_list: int32 [64, 24], P('dp'), may hold values from 0 to 23, each once within a row
- valid_tiles: int32 [64], P('dp'), may hold values from 2 to 24, as said below
- patch_weight: bfloat16 [768, 588], replicated, may hold values from -0.25 to 0.25
- norm_gain: float32 [768], replicated, may hold values from 0.25 to 1.75
- norm_bias: float32 [768], replicated, may hold values from -3 to 3
- w_query: bfloat16 [768, 768], replicated
- w_key: bfloat16 [768, 768], replicated
- w_value: bfloat16 [768, 768], replicated, may hold values from -0.21875 to 0.21875
- w_out: bfloat16 [768, 768], replicated, may hold values from -0.21875 to 0.21875
- cotangent: bfloat16 [64, 1536, 768], P('dp', 'seq'), may hold values from -16 to 16
Outputs:
- patch_grad: float32 [768, 588], P('dp')
Inputs may be any that keep to these rules, and one draw needn't show every extreme that they name: `tile_list`: each row is a permutation of the 24 storage indices. `valid_tiles`: some scene holds data in all 24 tiles and some in only 2.
All inputs are finite; a program needn't handle non-finite values.
Results may differ from a plain program's by a relative error of at most 0.012.
The roundings to bfloat16 on the way count: a program that leaves them out, or rounds other values in their place, can miss the bound.
Values may be sent and summed in bfloat16 or wider, within the bound.
No kernel may reach another device: no remote copies, remote signals or barrier semaphores. Data moves between devices by JAX's collectives and lax.ppermute only.
A program may use at most 32 MiB of HBM per device.

v0:
```python
import math

import jax
import jax.numpy as jnp
from jax import lax
from jax.sharding import PartitionSpec as P

HEADS = 12
HEAD_DIM = 64


eps_norm = 1e-06


def norm_forward(embedded, norm_gain, norm_bias):
    row_mean = jnp.mean(embedded, axis=-1, keepdims=True)
    centred = embedded - row_mean
    inv_std = lax.rsqrt(jnp.mean(centred * centred, axis=-1, keepdims=True) + eps_norm)
    normed = centred * inv_std
    return (normed, inv_std, (normed * norm_gain + norm_bias).astype(jnp.bfloat16))


def norm_backward(d_out, normed, inv_std, norm_gain):
    d_normed = d_out * norm_gain
    first_mean = jnp.mean(d_normed, axis=-1, keepdims=True)
    second_mean = jnp.mean(d_normed * normed, axis=-1, keepdims=True)
    return inv_std * (d_normed - first_mean - normed * second_mean)


def right_product(left, weight):
    return lax.dot_general(
        left, weight, (((1,), (1,)), ((), ())), preferred_element_type=jnp.float32
    )


def attend_heads(head_q, head_k, head_v, head_a, live_keys):
    seq_len = head_q.shape[0]
    block_len = math.gcd(seq_len, 512)
    blocks = seq_len // block_len
    inv_root = float(HEAD_DIM) ** (-0.5)
    query_blocks = head_q.reshape((blocks, block_len) + head_q.shape[1:])
    grad_blocks = head_a.reshape((blocks, block_len) + head_a.shape[1:])

    def one_block(carry, pair):
        key_acc, value_acc = carry
        q_block, a_block = pair
        scores = (
            jnp.einsum("qhd,khd->hqk", q_block, head_k, preferred_element_type=jnp.float32)
            * inv_root
        )
        scores = jnp.where(live_keys[None, None, :], scores, jnp.float32(-1e30))
        peak = jnp.max(scores, axis=-1, keepdims=True)
        expo = jnp.exp(scores - peak)
        probs = expo / jnp.sum(expo, axis=-1, keepdims=True)
        probs_low = probs.astype(jnp.bfloat16)
        d_probs = jnp.einsum("qhd,khd->hqk", a_block, head_v, preferred_element_type=jnp.float32)
        row_dot = jnp.sum(probs * d_probs, axis=-1, keepdims=True)
        d_scores = (probs * (d_probs - row_dot) * inv_root).astype(jnp.bfloat16)
        d_query = jnp.einsum(
            "hqk,khd->qhd", d_scores, head_k, preferred_element_type=jnp.float32
        ).astype(jnp.bfloat16)
        key_acc = key_acc + jnp.einsum(
            "hqk,qhd->khd", d_scores, q_block, preferred_element_type=jnp.float32
        )
        value_acc = value_acc + jnp.einsum(
            "hqk,qhd->khd", probs_low, a_block, preferred_element_type=jnp.float32
        )
        return ((key_acc, value_acc), d_query)

    zeros_acc = jnp.zeros(head_k.shape, jnp.float32)
    (key_acc, value_acc), query_parts = lax.scan(
        one_block, (zeros_acc, zeros_acc), (query_blocks, grad_blocks)
    )
    d_query = query_parts.reshape(head_q.shape)
    return (d_query, key_acc.astype(jnp.bfloat16), value_acc.astype(jnp.bfloat16))


def per_device(
    tiles,
    tile_list,
    valid_tiles,
    patch_weight,
    norm_gain,
    norm_bias,
    w_query,
    w_key,
    w_value,
    w_out,
    cotangent,
):
    position = lax.axis_index("seq")
    tiles_here = tiles.shape[1]
    tile_tok = tiles.shape[2]
    patch_in = tiles.shape[3]
    tok_rows = tiles_here * tile_tok
    wanted = lax.dynamic_slice_in_dim(tile_list[0], position * tiles_here, tiles_here)
    shard_piece = lax.all_gather(tiles, "seq", axis=1, tiled=True)
    row_count = shard_piece.shape[1]
    select = (wanted[:, None] == jnp.arange(row_count)[None, :]).astype(jnp.bfloat16)
    flat_piece = shard_piece[0].reshape(row_count, tile_tok * patch_in)
    arrived = jnp.dot(select, flat_piece, preferred_element_type=jnp.float32)
    patches = arrived.astype(jnp.bfloat16)
    patches = patches.reshape(tok_rows, patch_in)
    embedded = right_product(patches, patch_weight)
    normed, inv_std, ln_out = norm_forward(embedded, norm_gain, norm_bias)
    queries = jnp.dot(ln_out, w_query, preferred_element_type=jnp.float32).astype(jnp.bfloat16)
    key_rows = jnp.dot(ln_out, w_key, preferred_element_type=jnp.float32).astype(jnp.bfloat16)
    value_rows = jnp.dot(ln_out, w_value, preferred_element_type=jnp.float32).astype(jnp.bfloat16)
    limit = valid_tiles[0] * tile_tok
    live_rows = position * tok_rows + jnp.arange(tok_rows) < limit
    cot_rows = cotangent[0]
    cot_live = jnp.where(live_rows[:, None], cot_rows, jnp.zeros_like(cot_rows))
    d_attn = right_product(cot_live, w_out).astype(jnp.bfloat16)
    head_shape = (tok_rows, HEADS, HEAD_DIM)
    head_q, head_k, head_v, head_a = (
        lax.all_to_all(queries.reshape(head_shape), "seq", split_axis=1, concat_axis=0, tiled=True),
        lax.all_to_all(
            key_rows.reshape(head_shape), "seq", split_axis=1, concat_axis=0, tiled=True
        ),
        lax.all_to_all(
            value_rows.reshape(head_shape), "seq", split_axis=1, concat_axis=0, tiled=True
        ),
        lax.all_to_all(d_attn.reshape(head_shape), "seq", split_axis=1, concat_axis=0, tiled=True),
    )
    seq_len = head_q.shape[0]
    live_keys = jnp.arange(seq_len) < limit
    d_query, d_key, d_value = attend_heads(head_q, head_k, head_v, head_a, live_keys)
    back_q, back_k, back_v = (
        lax.all_to_all(d_query, "seq", split_axis=0, concat_axis=1, tiled=True),
        lax.all_to_all(d_key, "seq", split_axis=0, concat_axis=1, tiled=True),
        lax.all_to_all(d_value, "seq", split_axis=0, concat_axis=1, tiled=True),
    )
    inner = HEADS * HEAD_DIM
    d_ln = right_product(back_q.reshape(tok_rows, inner), w_query)
    d_ln = d_ln + right_product(back_k.reshape(tok_rows, inner), w_key)
    d_ln = d_ln + right_product(back_v.reshape(tok_rows, inner), w_value)
    d_embedded = (
        cot_live.astype(jnp.float32) + norm_backward(d_ln, normed, inv_std, norm_gain)
    ).astype(jnp.bfloat16)
    scale_grad = float(lax.axis_size("dp") * seq_len) ** (-0.5)
    partial_rows = lax.psum_scatter(
        lax.dot_general(
            d_embedded, patches, (((0,), (0,)), ((), ())), preferred_element_type=jnp.float32
        ),
        "dp",
        scatter_dimension=0,
        tiled=True,
    )
    summed = lax.psum(partial_rows, "seq")
    return summed * scale_grad


def solution(mesh):
    in_specs = (
        P("dp", "seq", None, None),
        P("dp", None),
        P("dp"),
        P(),
        P(),
        P(),
        P(),
        P(),
        P(),
        P(),
        P("dp", "seq", None),
    )
    out_specs = P("dp", None)
    return jax.shard_map(
        per_device, mesh=mesh, in_specs=in_specs, out_specs=out_specs, check_vma=False
    )
```

profile of v0, /device:TPU:16, one launch (start us, length us, event | category | flops | bytes accessed | tf_op | source)
XLA Modules:
  0.0 677.9 jit_solution(7759819540503955989)
XLA Ops:
  11.2 12.1 %all-to-all-start.2 = ((bf16[128,12,64]{0,2,1:T(8,128)(2,1)}), bf16[128,12,64]{0,2,1:T(8,128)(2,1)S(1)}, u32[]{:S(2)}, u32[]{:S(2)}) async-start(bf16[128,12,64]{0,2,1:T(8,128)(2,1)} %bitcast.10), calls=%async_computation.2 | async-start | bytes 393216 | tf_op jit(solution)/shard_map/all_to_all | solution.py:123
  23.4 63.2 %all-gather.2.cloned.1.call-done = bf16[1,24,64,588]{3,2,0,1:T(8,128)(2,1)} async-done(((bf16[1,2,64,588]{3,2,0,1:T(8,128)(2,1)}), bf16[1,24,64,588]{3,2,0,1:T(8,128)(2,1)}) %all-gather.2.cloned.1.call-update) | async-done | bytes 1806352 | tf_op jit(solution)/shard_map/all_gather | solution.py:97
  86.6 4.1 reshape_squeeze.3
  94.9 6.9 %all-to-all-start.3 = ((bf16[128,12,64]{0,2,1:T(8,128)(2,1)}), bf16[128,12,64]{0,2,1:T(8,128)(2,1)S(1)}, u32[]{:S(2)}, u32[]{:S(2)}) async-start(bf16[128,12,64]{0,2,1:T(8,128)(2,1)} %bitcast.13), calls=%async_computation.3 | async-start | bytes 393216 | tf_op jit(solution)/shard_map/all_to_all | solution.py:120
  103.0 11.1 %all-to-all-done.3 = bf16[128,12,64]{0,2,1:T(8,128)(2,1)S(1)} async-done(((bf16[128,12,64]{0,2,1:T(8,128)(2,1)}), bf16[128,12,64]{0,2,1:T(8,128)(2,1)S(1)}, u32[]{:S(2)}, u32[]{:S(2)}) %all-to-all-start.3) | async-done | bytes 196640 | tf_op jit(solution)/shard_map/all_to_all | solution.py:120
  114.8 3.7 all-to-all-start
  121.0 9.8 %all-to-all-done = bf16[128,12,64]{0,2,1:T(8,128)(2,1)S(1)} async-done(((bf16[128,12,64]{0,2,1:T(8,128)(2,1)}), bf16[128,12,64]{0,2,1:T(8,128)(2,1)S(1)}, u32[]{:S(2)}, u32[]{:S(2)}) %all-to-all-start) | async-done | bytes 196640 | tf_op jit(solution)/shard_map/all_to_all | solution.py:116
  131.5 4.3 all-to-all-start.1
  144.0 4.0 all-to-all-done.1
  149.0 32.7 %while.15 = (s32[]{:T(128)}, f32[1536,1,64]{0,2,1:T(8,128)S(1)}, f32[1536,1,64]{0,2,1:T(8,128)}, bf16[3,512,1,64]{1,3,2,0:T(8,128)(2,1)}, bf16[3,512,1,64]{1,3,2...) while((s32[]{:T(128)}, f32[1536,1,64]{0,2,1:T(8,128)S(1)}, ...), condition=%wide.region_6.7_spmd.clone, body=%wide.region_2.6_spmd.clone.sunk | while | flops 517898240 | bytes 55209172 | solution.py:71
  151.9 3.6 fusion.81
  162.8 3.6 fusion.81
  173.7 3.6 fusion.81
  184.9 9.8 %reduce.6 = bf16[1536,64]{1,0:T(8,128)(2,1)S(1)} reduce(bf16[1536,1,64]{2,1,0:T(2,128)(2,1)} %reshape.145, bf16[]{:T(256)} %broadcast.80), dimensions={1}, to_apply=%reshape.145.reduce_sub_computation | reduce | bytes 393218 | tf_op jit(solution)/shard_map/reshape | solution.py:74
  195.7 4.2 all-to-all-start.4
  201.8 10.4 %all-to-all-done.4 = bf16[12,2,4096]{2,1,0:T(2,128)(2,1)} async-done(((bf16[12,2,4096]{2,1,0:T(2,128)(2,1)}), bf16[12,2,4096]{2,1,0:T(2,128)(2,1)}, u32[]{:S(2)}, u32[]{:S(2)}) %all-to-all-start.4) | async-done | bytes 196640 | tf_op jit(solution)/shard_map/all_to_all | solution.py:129
  212.2 3.6 all-to-all-start.5
  218.7 9.4 %all-to-all-done.5 = bf16[12,2,4096]{2,1,0:T(2,128)(2,1)S(1)} async-done(((bf16[12,2,4096]{2,1,0:T(2,128)(2,1)}), bf16[12,2,4096]{2,1,0:T(2,128)(2,1)S(1)}, u32[]{:S(2)}, u32[]{:S(2)}) %all-to-all-start.5) | async-done | bytes 196640 | tf_op jit(solution)/shard_map/all_to_all | solution.py:130
  228.8 4.4 all-to-all-start.6
  244.0 2.2 fusion.42
  246.2 2.1 reshape.152
  254.1 259.6 %fusion.2 = f32[16,588]{1,0:T(8,128)S(1)} fusion(f32[768,588]{1,0:T(8,128)S(1)} %fusion.29), kind=kCustom, calls=%all-reduce-scatter | all-reduce-scatter fusion | flops 602113 | bytes 1848064
  513.7 26.3 %collective-permute-start.15 = (f32[12,588]{1,0:T(8,128)S(1)}, f32[12,588]{1,0:T(8,128)S(1)}, u32[]{:S(2)}, u32[]{:S(2)}) collective-permute-start(f32[12,588]{1,0:T(8,128)S(1)} %slice), channel_id=1, source_target_pairs={{0,192},{12,204},{24,216},{36,228},{48,240},{60,252},{72,264},{84,... | collective-permute-start | bytes 84680
  547.7 12.6 %collective-permute-start.12 = (f32[16,588]{1,0:T(8,128)S(1)}, f32[16,588]{1,0:T(8,128)S(1)}, u32[]{:S(2)}, u32[]{:S(2)}) collective-permute-start(f32[16,588]{1,0:T(8,128)S(1)} %fusion.2), channel_id=1, source_target_pairs={{0,156},{12,168},{24,180},{36,192},{48,204},{60,216},{72,228},{84,... | collective-permute-start | bytes 112904
  566.2 5.7 collective-permute-start.3
  571.9 7.2 %collective-permute-start.4 = (f32[16,588]{1,0:T(8,128)S(1)}, f32[16,588]{1,0:T(8,128)S(1)}, u32[]{:S(2)}, u32[]{:S(2)}) collective-permute-start(f32[16,588]{1,0:T(8,128)S(1)} %fusion.2), channel_id=1, source_target_pairs={{0,60},{12,72},{24,84},{36,96},{48,108},{60,120},{72,132},{84,144}... | collective-permute-start | bytes 112904
  579.1 7.0 %collective-permute-start.5 = (f32[16,588]{1,0:T(8,128)S(1)}, f32[16,588]{1,0:T(8,128)S(1)}, u32[]{:S(2)}, u32[]{:S(2)}) collective-permute-start(f32[16,588]{1,0:T(8,128)S(1)} %fusion.2), channel_id=1, source_target_pairs={{0,72},{12,84},{24,96},{36,108},{48,120},{60,132},{72,144},{84,156... | collective-permute-start | bytes 112904
  586.1 4.9 collective-permute-start.6
  598.8 10.3 %collective-permute-done.8 = f32[16,588]{1,0:T(8,128)S(1)} collective-permute-done((f32[16,588]{1,0:T(8,128)S(1)}, f32[16,588]{1,0:T(8,128)S(1)}, u32[]{:S(2)}, u32[]{:S(2)}) %collective-permute-start.8) | collective-permute-done | bytes 37664
  609.1 2.2 collective-permute-done.9
  611.3 2.7 concatenate
  614.1 56.3 %psum.7 = f32[12,588]{1,0:T(8,128)S(1)} all-reduce(f32[12,588]{1,0:T(8,128)S(1)} %constant_dynamic-slice_fusion), channel_id=1, replica_groups=mesh['dp'=64,'seq'=12] {'seq'}, use_global_device_ids=true, to_apply=%region_10.11 | all-reduce | flops 7056 | bytes 56448 | tf_op jit(solution)/shard_map/psum | solution.py:149
  (161 shorter events, 91.3 us)
Async XLA Ops:
  6.5 87.1 %copy-start = (bf16[768,768]{1,0:T(8,128)(2,1)S(1)}, bf16[768,768]{1,0:T(8,128)(2,1)}, u32[]{:S(2)}) copy-start(bf16[768,768]{1,0:T(8,128)(2,1)} %param.21) | copy-start | bytes 3538948
  6.5 16.8 %copy-start.20 = (s32[1,24]{1,0:T(1,128)S(1)}, s32[1,24]{1,0:T(1,128)}, u32[]{:S(2)}) copy-start(s32[1,24]{1,0:T(1,128)} %param.14) | copy-start | bytes 292
  6.5 80.0 %all-gather.2.cloned.1.call-start = ((), (), s32[]{:S(2)}) async-start(), calls=%async_computation.7 | async-start | bytes 2129920 | tf_op jit(solution)/shard_map/all_gather | solution.py:97
  11.2 83.7 %all-to-all-start.2 = ((bf16[128,12,64]{0,2,1:T(8,128)(2,1)}), bf16[128,12,64]{0,2,1:T(8,128)(2,1)S(1)}, u32[]{:S(2)}, u32[]{:S(2)}) async-start(bf16[128,12,64]{0,2,1:T(8,128)(2,1)} %bitcast.10), calls=%async_computation.2 | async-start | bytes 393216 | tf_op jit(solution)/shard_map/all_to_all | solution.py:123
  91.7 10.1 %copy-start.3 = (bf16[768,768]{1,0:T(8,128)(2,1)S(1)}, bf16[768,768]{1,0:T(8,128)(2,1)}, u32[]{:S(2)}) copy-start(bf16[768,768]{1,0:T(8,128)(2,1)} %param.19) | copy-start | bytes 3538948
  93.7 24.8 %copy-start.16 = (f32[128]{0:T(128)}, f32[128]{0:T(128)S(1)}, u32[]{:S(2)}) copy-start(f32[128]{0:T(128)S(1)} %add_rsqrt_fusion) | copy-start | bytes 1540
  94.9 25.3 %copy-start.7 = (bf16[128,12,64]{0,2,1:T(8,128)(2,1)}, bf16[128,12,64]{0,2,1:T(8,128)(2,1)S(1)}, u32[]{:S(2)}) copy-start(bf16[128,12,64]{0,2,1:T(8,128)(2,1)S(1)} %all-to-all-done.2) | copy-start | bytes 589828
  94.9 19.3 %all-to-all-start.3 = ((bf16[128,12,64]{0,2,1:T(8,128)(2,1)}), bf16[128,12,64]{0,2,1:T(8,128)(2,1)S(1)}, u32[]{:S(2)}, u32[]{:S(2)}) async-start(bf16[128,12,64]{0,2,1:T(8,128)(2,1)} %bitcast.13), calls=%async_computation.3 | async-start | bytes 393216 | tf_op jit(solution)/shard_map/all_to_all | solution.py:120
  114.8 16.0 %all-to-all-start = ((bf16[128,12,64]{0,2,1:T(8,128)(2,1)}), bf16[128,12,64]{0,2,1:T(8,128)(2,1)S(1)}, u32[]{:S(2)}, u32[]{:S(2)}) async-start(bf16[128,12,64]{0,2,1:T(8,128)(2,1)} %bitcast.4), calls=%async_computation | async-start | bytes 393216 | tf_op jit(solution)/shard_map/all_to_all | solution.py:116
  131.5 16.5 %all-to-all-start.1 = ((bf16[128,12,64]{0,2,1:T(8,128)(2,1)}), bf16[128,12,64]{0,2,1:T(8,128)(2,1)}, u32[]{:S(2)}, u32[]{:S(2)}) async-start(bf16[128,12,64]{0,2,1:T(8,128)(2,1)} %bitcast.7), calls=%async_computation.1 | async-start | bytes 393216 | tf_op jit(solution)/shard_map/all_to_all | solution.py:117
  195.7 16.5 %all-to-all-start.4 = ((bf16[12,2,4096]{2,1,0:T(2,128)(2,1)}), bf16[12,2,4096]{2,1,0:T(2,128)(2,1)}, u32[]{:S(2)}, u32[]{:S(2)}) async-start(bf16[12,2,4096]{2,1,0:T(2,128)(2,1)} %reshape.147), calls=%async_computation.4 | async-start | bytes 393216 | tf_op jit(solution)/shard_map/all_to_all | solution.py:129
  212.2 15.9 %all-to-all-start.5 = ((bf16[12,2,4096]{2,1,0:T(2,128)(2,1)}), bf16[12,2,4096]{2,1,0:T(2,128)(2,1)S(1)}, u32[]{:S(2)}, u32[]{:S(2)}) async-start(bf16[12,2,4096]{2,1,0:T(2,128)(2,1)} %reshape.149), calls=%async_computation.5 | async-start | bytes 393216 | tf_op jit(solution)/shard_map/all_to_all | solution.py:130
  228.8 17.4 %all-to-all-start.6 = ((bf16[12,2,4096]{2,1,0:T(2,128)(2,1)}), bf16[12,2,4096]{2,1,0:T(2,128)(2,1)}, u32[]{:S(2)}, u32[]{:S(2)}) async-start(bf16[12,2,4096]{2,1,0:T(2,128)(2,1)} %reshape.151), calls=%async_computation.6 | async-start | bytes 393216 | tf_op jit(solution)/shard_map/all_to_all | solution.py:131
  246.2 4.8 copy-start.4
  248.3 4.5 copy-start.17
  513.7 95.4 %copy-start.12 = (f32[16,588]{1,0:T(8,128)}, f32[16,588]{1,0:T(8,128)S(1)}, u32[]{:S(2)}) copy-start(f32[16,588]{1,0:T(8,128)S(1)} %fusion.2) | copy-start | bytes 112900
  513.7 34.0 %collective-permute-start.15 = (f32[12,588]{1,0:T(8,128)S(1)}, f32[12,588]{1,0:T(8,128)S(1)}, u32[]{:S(2)}, u32[]{:S(2)}) collective-permute-start(f32[12,588]{1,0:T(8,128)S(1)} %slice), channel_id=1, source_target_pairs={{0,192},{12,204},{24,216},{36,228},{48,240},{60,252},{72,264},{84,... | collective-permute-start | bytes 84680
  540.0 20.4 %collective-permute-start = (f32[16,588]{1,0:T(8,128)S(1)}, f32[16,588]{1,0:T(8,128)S(1)}, u32[]{:S(2)}, u32[]{:S(2)}) collective-permute-start(f32[16,588]{1,0:T(8,128)S(1)} %fusion.2), channel_id=1, source_target_pairs={{0,12},{12,24},{24,36},{36,48},{48,60},{60,72},{72,84},{84,96},{96... | collective-permute-start | bytes 112904
  541.9 20.4 %collective-permute-start.1 = (f32[16,588]{1,0:T(8,128)S(1)}, f32[16,588]{1,0:T(8,128)S(1)}, u32[]{:S(2)}, u32[]{:S(2)}) collective-permute-start(f32[16,588]{1,0:T(8,128)S(1)} %fusion.2), channel_id=1, source_target_pairs={{0,24},{12,36},{24,48},{36,60},{48,72},{60,84},{72,96},{84,108},{9... | collective-permute-start | bytes 112904
  543.9 20.4 %collective-permute-start.10 = (f32[16,588]{1,0:T(8,128)S(1)}, f32[16,588]{1,0:T(8,128)S(1)}, u32[]{:S(2)}, u32[]{:S(2)}) collective-permute-start(f32[16,588]{1,0:T(8,128)S(1)} %fusion.2), channel_id=1, source_target_pairs={{0,132},{12,144},{24,156},{36,168},{48,180},{60,192},{72,204},{84,... | collective-permute-start | bytes 112904
  545.8 20.4 %collective-permute-start.11 = (f32[16,588]{1,0:T(8,128)S(1)}, f32[16,588]{1,0:T(8,128)S(1)}, u32[]{:S(2)}, u32[]{:S(2)}) collective-permute-start(f32[16,588]{1,0:T(8,128)S(1)} %fusion.2), channel_id=1, source_target_pairs={{0,144},{12,156},{24,168},{36,180},{48,192},{60,204},{72,216},{84,... | collective-permute-start | bytes 112904
  547.7 24.2 %collective-permute-start.12 = (f32[16,588]{1,0:T(8,128)S(1)}, f32[16,588]{1,0:T(8,128)S(1)}, u32[]{:S(2)}, u32[]{:S(2)}) collective-permute-start(f32[16,588]{1,0:T(8,128)S(1)} %fusion.2), channel_id=1, source_target_pairs={{0,156},{12,168},{24,180},{36,192},{48,204},{60,216},{72,228},{84,... | collective-permute-start | bytes 112904
  560.4 18.7 %collective-permute-start.13 = (f32[16,588]{1,0:T(8,128)S(1)}, f32[16,588]{1,0:T(8,128)S(1)}, u32[]{:S(2)}, u32[]{:S(2)}) collective-permute-start(f32[16,588]{1,0:T(8,128)S(1)} %fusion.2), channel_id=1, source_target_pairs={{0,168},{12,180},{24,192},{36,204},{48,216},{60,228},{72,240},{84,... | collective-permute-start | bytes 112904
  562.3 23.8 %collective-permute-start.14 = (f32[16,588]{1,0:T(8,128)S(1)}, f32[16,588]{1,0:T(8,128)S(1)}, u32[]{:S(2)}, u32[]{:S(2)}) collective-permute-start(f32[16,588]{1,0:T(8,128)S(1)} %fusion.2), channel_id=1, source_target_pairs={{0,180},{12,192},{24,204},{36,216},{48,228},{60,240},{72,252},{84,... | collective-permute-start | bytes 112904
  564.3 26.8 %collective-permute-start.2 = (f32[16,588]{1,0:T(8,128)S(1)}, f32[16,588]{1,0:T(8,128)S(1)}, u32[]{:S(2)}, u32[]{:S(2)}) collective-permute-start(f32[16,588]{1,0:T(8,128)S(1)} %fusion.2), channel_id=1, source_target_pairs={{0,36},{12,48},{24,60},{36,72},{48,84},{60,96},{72,108},{84,120},{... | collective-permute-start | bytes 112904
  566.2 26.8 %collective-permute-start.3 = (f32[16,588]{1,0:T(8,128)S(1)}, f32[16,588]{1,0:T(8,128)S(1)}, u32[]{:S(2)}, u32[]{:S(2)}) collective-permute-start(f32[16,588]{1,0:T(8,128)S(1)} %fusion.2), channel_id=1, source_target_pairs={{0,48},{12,60},{24,72},{36,84},{48,96},{60,108},{72,120},{84,132},... | collective-permute-start | bytes 112904
  571.9 23.0 %collective-permute-start.4 = (f32[16,588]{1,0:T(8,128)S(1)}, f32[16,588]{1,0:T(8,128)S(1)}, u32[]{:S(2)}, u32[]{:S(2)}) collective-permute-start(f32[16,588]{1,0:T(8,128)S(1)} %fusion.2), channel_id=1, source_target_pairs={{0,60},{12,72},{24,84},{36,96},{48,108},{60,120},{72,132},{84,144}... | collective-permute-start | bytes 112904
  579.1 19.7 %collective-permute-start.5 = (f32[16,588]{1,0:T(8,128)S(1)}, f32[16,588]{1,0:T(8,128)S(1)}, u32[]{:S(2)}, u32[]{:S(2)}) collective-permute-start(f32[16,588]{1,0:T(8,128)S(1)} %fusion.2), channel_id=1, source_target_pairs={{0,72},{12,84},{24,96},{36,108},{48,120},{60,132},{72,144},{84,156... | collective-permute-start | bytes 112904
  586.1 12.6 %collective-permute-start.6 = (f32[16,588]{1,0:T(8,128)S(1)}, f32[16,588]{1,0:T(8,128)S(1)}, u32[]{:S(2)}, u32[]{:S(2)}) collective-permute-start(f32[16,588]{1,0:T(8,128)S(1)} %fusion.2), channel_id=1, source_target_pairs={{0,84},{12,96},{24,108},{36,120},{48,132},{60,144},{72,156},{84,16... | collective-permute-start | bytes 112904
  591.0 7.7 %collective-permute-start.7 = (f32[16,588]{1,0:T(8,128)S(1)}, f32[16,588]{1,0:T(8,128)S(1)}, u32[]{:S(2)}, u32[]{:S(2)}) collective-permute-start(f32[16,588]{1,0:T(8,128)S(1)} %fusion.2), channel_id=1, source_target_pairs={{0,96},{12,108},{24,120},{36,132},{48,144},{60,156},{72,168},{84,1... | collective-permute-start | bytes 112904
  593.0 16.1 %collective-permute-start.8 = (f32[16,588]{1,0:T(8,128)S(1)}, f32[16,588]{1,0:T(8,128)S(1)}, u32[]{:S(2)}, u32[]{:S(2)}) collective-permute-start(f32[16,588]{1,0:T(8,128)S(1)} %fusion.2), channel_id=1, source_target_pairs={{0,108},{12,120},{24,132},{36,144},{48,156},{60,168},{72,180},{84,... | collective-permute-start | bytes 112904
  594.9 16.4 %collective-permute-start.9 = (f32[16,588]{1,0:T(8,128)S(1)}, f32[16,588]{1,0:T(8,128)S(1)}, u32[]{:S(2)}, u32[]{:S(2)}) collective-permute-start(f32[16,588]{1,0:T(8,128)S(1)} %fusion.2), channel_id=1, source_target_pairs={{0,120},{12,132},{24,144},{36,156},{48,168},{60,180},{72,192},{84,... | collective-permute-start | bytes 112904
  (19 other events, 45.3 us)
Sparse Core Ops, SparseCore 0:
  9.7 76.7 all-gather.1
where the time goes:
time: 680 us; the launch traced here: 678 us
  blocking collectives  316 us (46%)
  starting transfers between devices  122 us (18%)
  waiting for transfers between devices  121 us (18%)
  local copies, waits for them, and re-layouts  50.7 us (7%)
  matrix products  34.8 us (5%)
  other arithmetic  17.5 us (3%)
  between operations  15.4 us (2%)
    unnamed x1, blocking collectives  260 us
    unnamed x16, starting transfers between devices  82.9 us
    all_gather x1, waiting for transfers between devices, per_device(): shard_piece = lax.all_gather(tiles, 'seq', axis=1, tiled=True)  63.2 us
    psum x1, blocking collectives, per_device(): summed = lax.psum(partial_rows, 'seq')  56.3 us
    unnamed x50, local copies, waits for them, and re-layouts  18.7 us
  transfers between devices with their start and end apart: 24, of which 8 were waited for; matrix products, arithmetic and copies ran while one was open for 6% of the time, Pallas kernels for 0%

commit v1 on v0

v1 whole, which is shorter than its diff:
```python
import jax
import jax.numpy as jnp
from jax import lax
from jax.experimental import pallas as pl
from jax.experimental.pallas import tpu as pltpu
from jax.sharding import Mesh
from jax.sharding import PartitionSpec as P

HEADS = 12
HEAD_DIM = 64
D = 768
PIX = 588
PIX_PAD = 640
TILES = 24
TILE_TOK = 64
SEQ = TILES * TILE_TOK
EPS = 1e-06
QB = 256
TOK_DEV = 128

DP_AXES = ("y", "zh", "x")
SEQ_AXES = ("zl", "core")


def dot(a, b, ca, cb):
    return lax.dot_general(
        a, b, (((ca,), (cb,)), ((), ())), preferred_element_type=jnp.float32
    )


def scene_kernel(
    list_ref, meta_ref, patch_ref, weight_ref, gain_ref, bias_ref, wqkv_ref, a_ref, cot_ref,
    out_ref,
    p_ref, normed_ref, istd_ref, q_ref, k_ref, v_ref, kt_ref, dqkv_ref, dk_ref, dv_ref, dt_ref,
):
    limit = meta_ref[0]
    position = meta_ref[1]

    def embed_block(c, carry):
        base = pl.multiple_of(c * QB, QB)
        for t in range(QB // TILE_TOK):
            tile = list_ref[c * (QB // TILE_TOK) + t]
            p_ref[pl.ds(base + t * TILE_TOK, TILE_TOK), :] = patch_ref[tile]
        embedded = dot(p_ref[pl.ds(base, QB), :], weight_ref[...], 1, 1)
        mean = jnp.sum(embedded, axis=1, keepdims=True) * (1.0 / D)
        centred = embedded - mean
        var = jnp.sum(centred * centred, axis=1, keepdims=True) * (1.0 / D)
        inv_std = lax.rsqrt(var + EPS)
        normed = centred * inv_std
        ln_out = (normed * gain_ref[...] + bias_ref[...]).astype(jnp.bfloat16)
        normed_ref[pl.ds(base, QB), :] = normed
        istd_ref[pl.ds(base, QB), :] = jnp.broadcast_to(inv_std, (QB, 128))
        qkv = dot(ln_out, wqkv_ref[...], 1, 0)
        q_ref[pl.ds(base, QB), :] = qkv[:, :HEAD_DIM].astype(jnp.bfloat16)
        k_ref[pl.ds(base, QB), :] = qkv[:, HEAD_DIM : 2 * HEAD_DIM].astype(jnp.bfloat16)
        v_ref[pl.ds(base, QB), :] = qkv[:, 2 * HEAD_DIM :].astype(jnp.bfloat16)
        return carry

    lax.fori_loop(0, SEQ // QB, embed_block, 0)
    kt_ref[...] = jnp.transpose(k_ref[...])
    dk_ref[...] = jnp.zeros_like(dk_ref)
    dv_ref[...] = jnp.zeros_like(dv_ref)
    inv_root = HEAD_DIM ** (-0.5)

    def attend_block(c, carry):
        base = pl.multiple_of(c * QB, QB)
        q_block = q_ref[pl.ds(base, QB), :]
        a_block = a_ref[pl.ds(base, QB), :]
        scores = dot(k_ref[...], q_block, 1, 1) * inv_root
        key_row = lax.broadcasted_iota(jnp.int32, (SEQ, QB), 0)
        scores = jnp.where(key_row < limit, scores, -1e30)
        peak = jnp.max(scores, axis=0, keepdims=True)
        expo = jnp.exp(scores - peak)
        probs = expo * (1.0 / jnp.sum(expo, axis=0, keepdims=True))
        d_probs = dot(v_ref[...], a_block, 1, 1)
        row_dot = jnp.sum(probs * d_probs, axis=0, keepdims=True)
        d_scores = (probs * (d_probs - row_dot) * inv_root).astype(jnp.bfloat16)
        dv_ref[...] += dot(probs.astype(jnp.bfloat16), a_block, 1, 0)
        dk_ref[...] += dot(d_scores, q_block, 1, 0)
        d_query = dot(kt_ref[...], d_scores, 1, 0)
        dqkv_ref[pl.ds(base, QB), :HEAD_DIM] = jnp.transpose(d_query).astype(jnp.bfloat16)
        return carry

    lax.fori_loop(0, SEQ // QB, attend_block, 0)
    dqkv_ref[:, HEAD_DIM : 2 * HEAD_DIM] = dk_ref[...].astype(jnp.bfloat16)
    dqkv_ref[:, 2 * HEAD_DIM :] = dv_ref[...].astype(jnp.bfloat16)

    def norm_block(c, carry):
        base = pl.multiple_of(c * TOK_DEV, TOK_DEV)
        d_ln = dot(dqkv_ref[pl.ds(base, TOK_DEV), :], wqkv_ref[...], 1, 1)
        g = d_ln * gain_ref[...]
        normed = normed_ref[pl.ds(base, TOK_DEV), :]
        first = jnp.sum(g, axis=1, keepdims=True) * (1.0 / D)
        second = jnp.sum(g * normed, axis=1, keepdims=True) * (1.0 / D)
        d_emb = istd_ref[pl.ds(base, TOK_DEV), :1] * (g - first - normed * second)
        own = jnp.where(c == position, 1.0, 0.0)
        d_emb = d_emb + cot_ref[...].astype(jnp.float32) * own
        dt_ref[:, pl.ds(base, TOK_DEV)] = jnp.transpose(d_emb).astype(jnp.bfloat16)
        return carry

    lax.fori_loop(0, SEQ // TOK_DEV, norm_block, 0)

    def grad_block(b, carry):
        rows = pl.multiple_of(b * 96, 96)
        part = dot(dt_ref[pl.ds(rows, 96), :], p_ref[...], 1, 0).astype(jnp.bfloat16)
        half = pl.multiple_of(b * 48, 48)
        out_ref[0, pl.ds(half, 48), :] = part[:48]
        out_ref[1, pl.ds(half, 48), :] = part[48:]
        return carry

    lax.fori_loop(0, D // 96, grad_block, 0)


def scene_call(order, meta, patches, weight, gain, bias, wqkv, head_a, cot_live):
    bf, f32 = jnp.bfloat16, jnp.float32
    smem = pl.BlockSpec(memory_space=pltpu.SMEM)
    vmem = pl.BlockSpec(memory_space=pltpu.VMEM)
    return pl.pallas_call(
        scene_kernel,
        out_shape=jax.ShapeDtypeStruct((2, D // 2, PIX_PAD), bf),
        in_specs=[smem, smem] + [vmem] * 7,
        out_specs=vmem,
        scratch_shapes=[
            pltpu.VMEM((SEQ, PIX_PAD), bf),
            pltpu.VMEM((SEQ, D), f32),
            pltpu.VMEM((SEQ, 128), f32),
            pltpu.VMEM((SEQ, HEAD_DIM), bf),
            pltpu.VMEM((SEQ, HEAD_DIM), bf),
            pltpu.VMEM((SEQ, HEAD_DIM), bf),
            pltpu.VMEM((HEAD_DIM, SEQ), bf),
            pltpu.VMEM((SEQ, 3 * HEAD_DIM), bf),
            pltpu.VMEM((SEQ, HEAD_DIM), f32),
            pltpu.VMEM((SEQ, HEAD_DIM), f32),
            pltpu.VMEM((D, SEQ), bf),
        ],
        compiler_params=pltpu.CompilerParams(vmem_limit_bytes=48 << 20),
    )(order, meta, patches, weight, gain, bias, wqkv, head_a, cot_live)


def exchange(x, axes):
    return lax.all_to_all(x, axes, 0, 0, tiled=True)


def gather(x, axes, count):
    copies = jnp.broadcast_to(x[None], (count,) + x.shape)
    return lax.all_to_all(copies, axes, 0, 0, tiled=False)


def per_device(
    tiles, tile_list, valid_tiles, patch_weight, norm_gain, norm_bias,
    w_query, w_key, w_value, w_out, cotangent,
):
    bf, f32 = jnp.bfloat16, jnp.float32
    position = lax.axis_index(SEQ_AXES)
    limit = valid_tiles[0] * TILE_TOK
    pixels = jnp.pad(tiles.reshape(TOK_DEV, PIX), ((0, 0), (0, PIX_PAD - PIX)))
    by_chip = gather(pixels, "zl", 6)
    patches = gather(by_chip.reshape(6 * TOK_DEV, PIX_PAD), "core", 2)
    patches = patches.reshape(2, 6, 2, TILE_TOK, PIX_PAD)

    live_rows = position * TOK_DEV + jnp.arange(TOK_DEV) < limit
    cot_rows = cotangent[0]
    cot_live = jnp.where(live_rows[:, None], cot_rows, jnp.zeros_like(cot_rows))
    d_attn = dot(cot_live, w_out, 1, 1).astype(bf)
    by_head = jnp.transpose(d_attn.reshape(TOK_DEV, HEADS, HEAD_DIM), (1, 0, 2))
    head_a = exchange(by_head, SEQ_AXES).reshape(SEQ, HEAD_DIM)

    start = position * HEAD_DIM
    wqkv = jnp.concatenate(
        [lax.dynamic_slice_in_dim(w, start, HEAD_DIM, 1) for w in (w_query, w_key, w_value)], axis=1
    )
    weight = jnp.pad(patch_weight, ((0, 0), (0, PIX_PAD - PIX)))
    stored = tile_list[0]
    chip = stored // 4
    place = (stored // 2) % 2 * 12 + chip * 2 + stored % 2
    meta = jnp.stack([limit, position])
    patches = patches.reshape(TILES, TILE_TOK, PIX_PAD)
    halves = scene_call(
        place, meta, patches, weight, norm_gain[None], norm_bias[None], wqkv, head_a, cot_live
    )

    pair = exchange(halves, "core")
    mine = (pair[0].astype(f32) + pair[1].astype(f32)).astype(bf)
    along_y = exchange(mine.reshape(8, 48, PIX_PAD), "y")
    row_sum = jnp.sum(along_y.astype(f32), axis=0).astype(bf)
    along_x = exchange(row_sum.reshape(4, 12, PIX_PAD), "x")
    column = jnp.sum(along_x.astype(f32), axis=0).astype(bf)
    along_z = gather(column, ("zh", "zl"), 12)
    total = jnp.sum(along_z.astype(f32), axis=0)
    other = lax.ppermute(total, "core", [(0, 1), (1, 0)])
    same = lax.axis_index("core") == lax.axis_index("zh")
    result = jnp.where(same, total, other)[:, :PIX]
    return result * (float(64 * SEQ) ** (-0.5))


def solution(mesh):
    fine = Mesh(mesh.devices.reshape(8, 2, 4, 6, 2), ("y", "zh", "x", "zl", "core"))
    in_specs = (
        P(DP_AXES, SEQ_AXES, None, None), P(DP_AXES, None), P(DP_AXES),
        P(), P(), P(), P(), P(), P(), P(), P(DP_AXES, SEQ_AXES, None),
    )
    return jax.shard_map(
        per_device, mesh=fine, in_specs=in_specs, out_specs=P(DP_AXES, None), check_vma=False
    )
```

time: 680 us -> 172 us (0.25)
  the two profiles are of different devices: /device:TPU:16 before, /device:TPU:1 now
where the time goes in v1:
time: 172 us; the launch traced here: 171 us
  blocking collectives  62.1 us (36%)
  waiting for transfers between devices  42.8 us (25%)
  Pallas kernels  29.7 us (17%)
  starting transfers between devices  25.8 us (15%)
  local copies, waits for them, and re-layouts  7.12 us (4%)
  other arithmetic  2.2 us (1%)
    all_to_all x3, blocking collectives, exchange(): return lax.all_to_all(x, axes, 0, 0, tiled=True)  35.1 us
    all_to_all x1, waiting for transfers between devices, gather(): return lax.all_to_all(copies, axes, 0, 0, tiled=False)  29.9 us
    pallas_call x1, Pallas kernels, scene_call(): pl.pallas_call(scene_kernel, out_shape=jax.ShapeDtypeStruct((2, D // 2, P...  29.7 us
    all_to_all x2, blocking collectives, gather(): return lax.all_to_all(copies, axes, 0, 0, tiled=False)  27 us
    all_to_all x1, starting transfers between devices, exchange(): return lax.all_to_all(x, axes, 0, 0, tiled=True)  13.9 us
    all_to_all x1, waiting for transfers between devices, exchange(): return lax.all_to_all(x, axes, 0, 0, tiled=True)  12 us
    ppermute x1, starting transfers between devices, per_device(): other = lax.ppermute(total, 'core', [(0, 1), (1, 0)])  7.62 us
    all_to_all x1, starting transfers between devices, gather(): return lax.all_to_all(copies, axes, 0, 0, tiled=False)  4.36 us
  transfers between devices with their start and end apart: 3, of which 3 were waited for; matrix products, arithmetic and copies ran while one was open for 2% of the time, Pallas kernels for 0%

profile of v1, /device:TPU:1, one launch (start us, length us, event | category | flops | bytes accessed | tf_op | source)
XLA Modules:
  0.0 171.2 jit_solution(16144059637088348667)
XLA Ops:
  0.8 1.0 bitcast_select_fusion.cot_ref
  1.8 0.0 copy-start.2
  1.8 0.5 convolution_convert_fusion
  2.4 0.8 copy.18
  3.2 13.9 %all-to-all-start.2 = ((bf16[12,128,64]{1,2,0:T(8,128)(2,1)}), bf16[12,128,64]{1,2,0:T(8,128)(2,1)S(1)}, u32[]{:S(2)}, u32[]{:S(2)}) async-start(bf16[12,128,64]{1,2,0:T(8,128)(2,1)} %bitcast.8), calls=%async_computation.2 | async-start | bytes 393216 | tf_op jit(solution)/shard_map/all_to_all | solution.py:141
  17.0 12.0 %all-to-all-done.2 = bf16[12,128,64]{1,2,0:T(8,128)(2,1)S(1)} async-done(((bf16[12,128,64]{1,2,0:T(8,128)(2,1)}), bf16[12,128,64]{1,2,0:T(8,128)(2,1)S(1)}, u32[]{:S(2)}, u32[]{:S(2)}) %all-to-all-start.2) | async-done | bytes 196640 | tf_op jit(solution)/shard_map/all_to_all | solution.py:141
  29.0 1.1 broadcast_in_dim.37
  30.1 4.4 %all-to-all-start = ((bf16[6,128,640]{2,1,0:T(8,128)(2,1)}), bf16[6,128,640]{2,1,0:T(8,128)(2,1)}, u32[]{:S(2)}, u32[]{:S(2)}) async-start(bf16[6,128,640]{2,1,0:T(8,128)(2,1)} %broadcast_in_dim.37), calls=%async_computation | async-start | bytes 1966080 | tf_op jit(solution)/shard_map/all_to_all | solution.py:146
  34.5 0.6 copy.17
  35.1 0.0 copy-start.3
  35.2 0.0 copy-start.4
  35.2 0.1 pad.9.weight_ref
  35.3 0.6 copy-done.3
  35.8 0.0 copy-done.4
  35.9 0.1 pad_add_fusion.meta_ref
  35.9 1.0 constant_dynamic-slice_fusion.2
  37.0 1.2 constant_dynamic-slice_fusion
  38.2 0.2 pad_maximum_fusion.wqkv_ref
  38.5 0.2 copy.19
  38.7 29.9 %all-to-all-done = bf16[6,128,640]{2,1,0:T(8,128)(2,1)} async-done(((bf16[6,128,640]{2,1,0:T(8,128)(2,1)}), bf16[6,128,640]{2,1,0:T(8,128)(2,1)}, u32[]{:S(2)}, u32[]{:S(2)}) %all-to-all-start) | async-done | bytes 983072 | tf_op jit(solution)/shard_map/all_to_all | solution.py:146
  68.6 1.4 broadcast_in_dim.39
  70.0 6.3 %all_to_all.35 = bf16[2,768,640]{2,1,0:T(8,128)(2,1)S(1)} all-to-all(bf16[2,768,640]{2,1,0:T(8,128)(2,1)S(1)} %broadcast_in_dim.39), channel_id=1, replica_groups=mesh['y'=8,'zh'=2,'x'=4,'zl'=6,'core'=2] {'core'}, dimensions={0} | all-to-all | bytes 3932160 | tf_op jit(solution)/shard_map/all_to_all | solution.py:146
  76.3 29.7 %shard_map.109 = bf16[2,384,640]{2,1,0:T(8,128)(2,1)S(1)} custom-call(s32[24]{0:T(128)S(1)} %fusion.1.list_ref, s32[2]{0:T(128)S(1)} %pad_add_fusion.meta_ref, bf16[24,64,640]{2,1,0:T(8,128)(2,1)S(1)} %bitcast.30, bf16[768,640]{1,0:T(8,128)(2,1)S(1)} %pad.9.weight_ref, f32[1,768]{1,0:T(1,128)S(1)} %broadcast_in_dim.40.gain_ref, ...), custom_call_target="tpu_custom_call" | custom-call | tf_op jit(solution)/shard_map/pallas_call | solution.py:118
  106.0 4.5 %all_to_all.36 = bf16[2,384,640]{2,1,0:T(8,128)(2,1)S(1)} all-to-all(bf16[2,384,640]{2,1,0:T(8,128)(2,1)S(1)} %shard_map.109), channel_id=1, replica_groups=mesh['y'=8,'zh'=2,'x'=4,'zl'=6,'core'=2] {'core'}, dimensions={0} | all-to-all | bytes 1966080 | tf_op jit(solution)/shard_map/all_to_all | solution.py:141
  110.5 0.1 add_convert_fusion
  110.6 22.2 %all_to_all.37 = bf16[8,48,640]{2,1,0:T(8,128)(2,1)S(1)} all-to-all(bf16[8,48,640]{2,1,0:T(8,128)(2,1)S(1)} %bitcast.32), channel_id=1, replica_groups=mesh['y'=8,'zh'=2,'x'=4,'zl'=6,'core'=2] {'y'}, dimensions={0} | all-to-all | bytes 983040 | tf_op jit(solution)/shard_map/all_to_all | solution.py:141
  132.9 0.1 reduce_sum.33
  133.0 8.4 %all_to_all.38 = bf16[4,12,640]{2,1,0:T(8,128)(2,1)S(1)} all-to-all(bf16[4,12,640]{2,1,0:T(8,128)(2,1)S(1)} %reshape.33), channel_id=1, replica_groups=mesh['y'=8,'zh'=2,'x'=4,'zl'=6,'core'=2] {'x'}, dimensions={0} | all-to-all | bytes 122880 | tf_op jit(solution)/shard_map/all_to_all | solution.py:141
  141.4 20.7 %all_to_all.39 = bf16[12,12,640]{2,1,0:T(8,128)(2,1)S(1)} all-to-all(bf16[12,12,640]{2,1,0:T(8,128)(2,1)S(1)} %broadcast_in_dim.44), channel_id=1, replica_groups=mesh['y'=8,'zh'=2,'x'=4,'zl'=6,'core'=2] {'zh','zl'}, dimensions={0} | all-to-all | bytes 368640 | tf_op jit(solution)/shard_map/all_to_all | solution.py:146
  162.1 7.6 %collective-permute-start = (f32[12,640]{1,0:T(8,128)S(1)}, f32[12,640]{1,0:T(8,128)S(1)}, u32[]{:S(2)}, u32[]{:S(2)}) collective-permute-start(f32[12,640]{1,0:T(8,128)S(1)} %convert_reduce_fusion), channel_id=1, source_target_pairs={{0,1},{1,0},{2,3},{3,2},{4,5},{5,4},{6,7},{7,6},{8,9},{9,8},{10,11... | collective-permute-start | bytes 92168 | tf_op jit(solution)/shard_map/ppermute | solution.py:190
  169.8 0.8 collective-permute-done
  170.6 0.6 fusion
  (16 shorter events, 0.2 us)
Async XLA Ops:
  0.0 1.8 %copy-start = (bf16[768,768]{1,0:T(8,128)(2,1)S(1)}, bf16[768,768]{1,0:T(8,128)(2,1)}, u32[]{:S(2)}) copy-start(bf16[768,768]{1,0:T(8,128)(2,1)} %param.20) | copy-start | bytes 3538948
  1.8 15.2 %copy-start.2 = (bf16[1,2,64,588]{3,2,1,0:T(8,128)(2,1)S(1)}, bf16[1,2,64,588]{3,2,1,0:T(8,128)(2,1)}, u32[]{:S(2)}) copy-start(bf16[1,2,64,588]{3,2,1,0:T(8,128)(2,1)} %param.11) | copy-start | bytes 451588
  3.2 25.9 %all-to-all-start.2 = ((bf16[12,128,64]{1,2,0:T(8,128)(2,1)}), bf16[12,128,64]{1,2,0:T(8,128)(2,1)S(1)}, u32[]{:S(2)}, u32[]{:S(2)}) async-start(bf16[12,128,64]{1,2,0:T(8,128)(2,1)} %bitcast.8), calls=%async_computation.2 | async-start | bytes 393216 | tf_op jit(solution)/shard_map/all_to_all | solution.py:141
  30.1 4.4 %copy-start.1 = (bf16[768,588]{0,1:T(8,128)(2,1)S(1)}, bf16[768,588]{0,1:T(8,128)(2,1)}, u32[]{:S(2)}) copy-start(bf16[768,588]{0,1:T(8,128)(2,1)} %param.14) | copy-start | bytes 2709508
  30.1 38.5 %all-to-all-start = ((bf16[6,128,640]{2,1,0:T(8,128)(2,1)}), bf16[6,128,640]{2,1,0:T(8,128)(2,1)}, u32[]{:S(2)}, u32[]{:S(2)}) async-start(bf16[6,128,640]{2,1,0:T(8,128)(2,1)} %broadcast_in_dim.37), calls=%async_computation | async-start | bytes 1966080 | tf_op jit(solution)/shard_map/all_to_all | solution.py:146
  35.1 0.7 copy-start.3
  35.2 0.7 copy-start.4
  35.8 2.6 %copy-start.5 = (s32[1,24]{1,0:T(1,128)S(1)}, s32[1,24]{1,0:T(1,128)}, u32[]{:S(2)}) copy-start(s32[1,24]{1,0:T(1,128)} %param.12) | copy-start | bytes 292
  162.1 8.5 %collective-permute-start = (f32[12,640]{1,0:T(8,128)S(1)}, f32[12,640]{1,0:T(8,128)S(1)}, u32[]{:S(2)}, u32[]{:S(2)}) collective-permute-start(f32[12,640]{1,0:T(8,128)S(1)} %convert_reduce_fusion), channel_id=1, source_target_pairs={{0,1},{1,0},{2,3},{3,2},{4,5},{5,4},{6,7},{7,6},{8,9},{9,8},{10,11... | collective-permute-start | bytes 92168 | tf_op jit(solution)/shard_map/ppermute | solution.py:190

commit v2 on v1

v2 whole, which is shorter than its diff:
```python
import jax
import jax.numpy as jnp
from jax import lax
from jax.experimental import pallas as pl
from jax.experimental.pallas import tpu as pltpu
from jax.sharding import Mesh
from jax.sharding import PartitionSpec as P

HEADS = 12
HEAD_DIM = 64
D = 768
PIX = 588
PIX_ROW = 592
PIX_PAD = 640
TILES = 24
TILE_TOK = 64
SEQ = TILES * TILE_TOK
HALF = SEQ // 2
EPS = 1e-06
QB = 256
TOK_DEV = 128
EMBED_VMEM = 12 << 20
SCENE_VMEM = 38 << 20

DP_AXES = ("y", "zh", "x")
CHIP_AXES = ("zt", "zi")
SEQ_AXES = ("zt", "zi", "core")


def dot(a, b, ca, cb):
    return lax.dot_general(
        a, b, (((ca,), (cb,)), ((), ())), preferred_element_type=jnp.float32
    )


WQKV = slice(TOK_DEV, TOK_DEV + 3 * HEAD_DIM)
FEATURES = [slice(r * 128, (r + 1) * 128) for r in range(D // 128)]
KEYS = [slice(r * 128, (r + 1) * 128) for r in range(SEQ // 128)]


def wide(x):
    return jnp.concatenate([x, x], axis=1)


def join_blocks(own_ref, other_ref, pixel_ref):
    for b in range(6):
        block = own_ref[b] if b < 3 else other_ref[b - 3]
        pixel_ref[:PIX_ROW, b * 128 : (b + 1) * 128] = block
    pixel_ref[PIX_ROW:, :] = jnp.zeros((PIX_PAD - PIX_ROW, HALF), jnp.bfloat16)


def fold(x):
    return jnp.sum(x.reshape(x.shape[0] // 8, 8, x.shape[1]), axis=0)


def normalise(emb_ref, ln_ref, affine_ref):
    total = sum(fold(emb_ref[rows, :]) for rows in FEATURES)
    mean = jnp.sum(total, axis=0, keepdims=True) * (1.0 / D)
    squares = jnp.zeros((8, QB), jnp.float32)
    for rows in FEATURES:
        centred = emb_ref[rows, :] - mean
        squares = squares + fold(centred * centred)
    var = jnp.sum(squares, axis=0, keepdims=True) * (1.0 / D)
    inv_std = lax.rsqrt(var + EPS)
    for rows in FEATURES:
        normed = (emb_ref[rows, :] - mean) * inv_std
        emb_ref[rows, :] = normed
        ln_out = normed * wide(affine_ref[0, rows, :]) + wide(affine_ref[1, rows, :])
        ln_ref[rows, :] = ln_out.astype(jnp.bfloat16)
    return mean, inv_std


def start_loads(sources, targets, sems):
    copies = [
        pltpu.make_async_copy(source, target, sems.at[i])
        for i, (source, target) in enumerate(zip(sources, targets, strict=True))
    ]
    for copy in copies:
        copy.start()
    return copies


def embed_kernel(
    own_hbm, other_hbm, weight_hbm, pack_hbm, affine_hbm,
    mean_ref, istd_ref, qkv_ref, pixel_ref, emb_ref, ln_ref,
    own_ref, other_ref, weight_ref, pack_ref, affine_ref, sems, wqkv_t_ref,
):
    loads = start_loads(
        (own_hbm, other_hbm, weight_hbm, pack_hbm, affine_hbm),
        (own_ref, other_ref, weight_ref, pack_ref, affine_ref),
        sems,
    )
    for load in loads:
        load.wait()
    wqkv_t_ref[...] = jnp.transpose(pack_ref[:, WQKV])
    join_blocks(own_ref, other_ref, pixel_ref)
    chunks = [slice(c * QB, (c + 1) * QB) for c in range(HALF // QB)]
    for c, at in enumerate(chunks):
        emb_ref[c] = dot(weight_ref[...], pixel_ref[:, at], 1, 0)
    for c, at in enumerate(chunks):
        mean, inv_std = normalise(emb_ref.at[c], ln_ref.at[c], affine_ref)
        mean_ref[:, at] = mean
        istd_ref[:, at] = inv_std
        qkv_ref[:, at] = dot(wqkv_t_ref[...], ln_ref[c], 1, 0).astype(jnp.bfloat16)


def embed_call(own, other, weight, affine, packed):
    bf, f32 = jnp.bfloat16, jnp.float32
    vmem = pl.BlockSpec(memory_space=pltpu.VMEM)
    return pl.pallas_call(
        embed_kernel,
        out_shape=(
            jax.ShapeDtypeStruct((1, HALF), f32),
            jax.ShapeDtypeStruct((1, HALF), f32),
            jax.ShapeDtypeStruct((3 * HEAD_DIM, HALF), bf),
        ),
        in_specs=[pl.BlockSpec(memory_space=pl.ANY)] * 5,
        out_specs=(vmem,) * 3,
        scratch_shapes=[
            pltpu.VMEM((PIX_PAD, HALF), bf),
            pltpu.VMEM((HALF // QB, D, QB), f32),
            pltpu.VMEM((HALF // QB, D, QB), bf),
            *(pltpu.VMEM(x.shape, x.dtype) for x in (own, other, weight, packed, affine)),
            pltpu.SemaphoreType.DMA((5,)),
            pltpu.VMEM((3 * HEAD_DIM, D), bf),
        ],
        compiler_params=pltpu.CompilerParams(vmem_limit_bytes=EMBED_VMEM),
    )(own, other, weight, packed, affine)


def scene_kernel(
    place_ref, meta_ref, mean_a, istd_a, qkv_a,
    far_own_hbm, far_other_hbm, weight_hbm, pack_hbm, affine_hbm,
    near_own_hbm, near_other_hbm, head_hbm,
    keep_ref, send_ref,
    far_own, far_other, weight_ref, pack_ref, affine_ref,
    near_own, near_other, head_ref, sems, wqkv_t_ref,
    pix_a, pix_b, emb_ref, istd_b, qkv_b,
    k_ref, v_ref, kt_ref, qt_ref, q_ref, a_ref, live_ref, dqkv_ref, dk_ref, dv_ref, dt_ref,
    pick_ref, grad_ref, s_ref, dp_ref, p_ref, ds_ref, ln_ref, g_ref,
):
    bf, f32 = jnp.bfloat16, jnp.float32
    valid, position, core = meta_ref[0], meta_ref[1], meta_ref[2]
    inv_root = HEAD_DIM ** (-0.5)
    half_chunks = [slice(c * QB, (c + 1) * QB) for c in range(HALF // QB)]
    chunks = [slice(c * QB, (c + 1) * QB) for c in range(SEQ // QB)]
    steps = len(chunks)

    loads = start_loads(
        (far_own_hbm, far_other_hbm, weight_hbm, pack_hbm, affine_hbm,
         near_own_hbm, near_other_hbm, head_hbm),
        (far_own, far_other, weight_ref, pack_ref, affine_ref,
         near_own, near_other, head_ref),
        sems,
    )
    for load in loads[:3]:
        load.wait()
    join_blocks(far_own, far_other, pix_b)
    for c, at in enumerate(half_chunks):
        emb_ref[c] = dot(weight_ref[...], pix_b[:, at], 1, 0)
    for load in loads[3:]:
        load.wait()
    wqkv_t_ref[...] = jnp.transpose(pack_ref[:, WQKV])
    join_blocks(near_own, near_other, pix_a)
    for b in range(HEADS):
        rows = jnp.transpose(head_ref[b])
        for i in range(2):
            j = 2 * b + i
            base = pl.multiple_of(place_ref[j] * TILE_TOK, TILE_TOK)
            a_ref[pl.ds(base, TILE_TOK), :] = rows[i * TILE_TOK : (i + 1) * TILE_TOK]
            live_ref[pl.ds(base, TILE_TOK), :] = jnp.full(
                (TILE_TOK, 128), jnp.where(j < valid, 1.0, 0.0), f32
            )
    for c, at in enumerate(half_chunks):
        mean, inv_std = normalise(emb_ref.at[c], ln_ref.at[c], affine_ref)
        istd_b[:, at] = inv_std
        qkv_b[:, at] = dot(wqkv_t_ref[...], ln_ref[c], 1, 0).astype(bf)

    for i, qkv in enumerate((qkv_a, qkv_b)):
        at = slice(i * HALF, (i + 1) * HALF)
        qt_ref[:, at] = qkv[:HEAD_DIM, :] * jnp.asarray(inv_root, bf)
        kt_ref[:, at] = qkv[HEAD_DIM : 2 * HEAD_DIM, :]
        kv = jnp.transpose(qkv[HEAD_DIM:, :])
        k_ref[at, :] = kv[:, :HEAD_DIM]
        v_ref[at, :] = kv[:, HEAD_DIM:]
    q_ref[...] = jnp.transpose(qt_ref[...])

    def scores_of(c):
        s_ref[c % 2] = dot(k_ref[...], qt_ref[:, chunks[c]], 1, 0)
        dp_ref[c % 2] = dot(v_ref[...], a_ref[chunks[c], :], 1, 1)

    def softmax_of(c):
        scores, d_probs = s_ref.at[c % 2], dp_ref.at[c % 2]
        peak = jnp.full((8, QB), -1e30, f32)
        for rows in KEYS:
            masked = jnp.where(wide(live_ref[rows, :]) > 0.5, scores[rows, :], -1e30)
            peak = jnp.maximum(peak, jnp.max(masked.reshape(16, 8, QB), axis=0))
        peak = jnp.max(peak, axis=0, keepdims=True)
        total = jnp.zeros((8, QB), f32)
        weighted = jnp.zeros((8, QB), f32)
        for rows in KEYS:
            masked = jnp.where(wide(live_ref[rows, :]) > 0.5, scores[rows, :], -1e30)
            expo = jnp.exp(masked - peak)
            scores[rows, :] = expo
            total = total + fold(expo)
            weighted = weighted + fold(expo * d_probs[rows, :])
        scale = 1.0 / jnp.sum(total, axis=0, keepdims=True)
        row_dot = jnp.sum(weighted, axis=0, keepdims=True) * scale
        for rows in KEYS:
            probs = scores[rows, :] * scale
            p_ref[c % 2, rows, :] = probs.astype(bf)
            ds_ref[c % 2, rows, :] = (probs * (d_probs[rows, :] - row_dot)).astype(bf)

    def grads_of(c):
        d_value = dot(p_ref[c % 2], a_ref[chunks[c], :], 1, 0)
        d_key = dot(ds_ref[c % 2], q_ref[chunks[c], :], 1, 0)
        dv_ref[...] = d_value if c == 0 else dv_ref[...] + d_value
        dk_ref[...] = d_key if c == 0 else dk_ref[...] + d_key
        d_query = dot(kt_ref[...], ds_ref[c % 2], 1, 0) * inv_root
        dqkv_ref[:HEAD_DIM, chunks[c]] = d_query.astype(bf)

    scores_of(0)
    for c in range(steps):
        if c + 1 < steps:
            scores_of(c + 1)
        if c > 0:
            grads_of(c - 1)
        softmax_of(c)
    grads_of(steps - 1)
    dqkv_ref[HEAD_DIM : 2 * HEAD_DIM, :] = jnp.transpose(dk_ref[...]).astype(bf)
    dqkv_ref[2 * HEAD_DIM :, :] = jnp.transpose(dv_ref[...]).astype(bf)

    def norm_grad(c, normed_ref, inv_std):
        slot = c % 2
        g_ref[slot] = dot(pack_ref[:, WQKV], dqkv_ref[:, chunks[c]], 1, 0)
        first = jnp.zeros((8, QB), f32)
        second = jnp.zeros((8, QB), f32)
        for rows in FEATURES:
            g = g_ref[slot, rows, :] * wide(affine_ref[0, rows, :])
            g_ref[slot, rows, :] = g
            first = first + fold(g)
            second = second + fold(g * normed_ref[rows, :])
        first = jnp.sum(first, axis=0, keepdims=True) * (1.0 / D)
        second = jnp.sum(second, axis=0, keepdims=True) * (1.0 / D)
        for rows in FEATURES:
            d_emb = inv_std * (g_ref[slot, rows, :] - first - normed_ref[rows, :] * second)
            dt_ref[rows, chunks[c]] = d_emb.astype(bf)

    for c, at in enumerate(half_chunks):
        norm_grad(c + steps // 2, emb_ref.at[c], istd_b[:, at])
    for c, at in enumerate(half_chunks):
        emb_ref[c] = dot(weight_ref[...], pix_a[:, at], 1, 0)
    grad_ref[...] = dot(dt_ref[:, HALF:], pix_b[...], 1, 1)
    for c, at in enumerate(half_chunks):
        mean, inv_std = mean_a[:, at], istd_a[:, at]
        for rows in FEATURES:
            emb_ref[c, rows, :] = (emb_ref[c, rows, :] - mean) * inv_std
        norm_grad(c, emb_ref.at[c], inv_std)

    lane = lax.broadcasted_iota(jnp.int32, (PIX_PAD, 128), 1)
    for i in range(2):
        spot = place_ref[2 * position + i]
        block = lax.div(spot, 2)
        base = pl.multiple_of(lax.rem(block, 6) * 128, 128)

        def fill(source):
            picked = source[:, pl.ds(base, 128)].astype(f32)
            turned = pltpu.roll(picked, TILE_TOK, 1)
            picked = jnp.where(lax.rem(spot, 2) == i, picked, turned)
            own = (lane < TILE_TOK) if i == 0 else (lane >= TILE_TOK)
            pick_ref[...] = jnp.where(own, picked, pick_ref[...])

        @pl.when(block < 6)
        def _():
            fill(pix_a)

        @pl.when(block >= 6)
        def _():
            fill(pix_b)

    grad_ref[...] += dot(dt_ref[:, :HALF], pix_a[...], 1, 1) + dot(
        pack_ref[:, :TOK_DEV], pick_ref[...].astype(bf), 1, 1
    )
    first_core = core == 0
    for y in range(8):
        for zh in range(2):
            for x in range(4):
                row, spot = 96 * y + 48 * zh + 12 * x, 12 * y + 6 * zh
                low, high = grad_ref[row : row + 6, :], grad_ref[row + 6 : row + 12, :]
                keep_ref[x, spot : spot + 6, :] = jnp.where(first_core, low, high)
                send_ref[x, spot : spot + 6, :] = jnp.where(first_core, high, low).astype(bf)


def scene_call(place, meta, near, far, front, head_t, weight, packed, affine):
    bf, f32 = jnp.bfloat16, jnp.float32
    smem = pl.BlockSpec(memory_space=pltpu.SMEM)
    vmem = pl.BlockSpec(memory_space=pltpu.VMEM)
    loaded = (*far, weight, packed, affine, *near, head_t)
    return pl.pallas_call(
        scene_kernel,
        out_shape=(
            jax.ShapeDtypeStruct((4, 96, PIX_PAD), f32),
            jax.ShapeDtypeStruct((4, 96, PIX_PAD), bf),
        ),
        in_specs=[smem, smem] + [vmem] * 3 + [pl.BlockSpec(memory_space=pl.ANY)] * 8,
        out_specs=(vmem, vmem),
        scratch_shapes=[
            *(pltpu.VMEM(x.shape, x.dtype) for x in loaded),
            pltpu.SemaphoreType.DMA((8,)),
            pltpu.VMEM((3 * HEAD_DIM, D), bf),
            pltpu.VMEM((PIX_PAD, HALF), bf),
            pltpu.VMEM((PIX_PAD, HALF), bf),
            pltpu.VMEM((HALF // QB, D, QB), f32),
            pltpu.VMEM((1, HALF), f32),
            pltpu.VMEM((3 * HEAD_DIM, HALF), bf),
            pltpu.VMEM((SEQ, HEAD_DIM), bf),
            pltpu.VMEM((SEQ, HEAD_DIM), bf),
            pltpu.VMEM((HEAD_DIM, SEQ), bf),
            pltpu.VMEM((HEAD_DIM, SEQ), bf),
            pltpu.VMEM((SEQ, HEAD_DIM), bf),
            pltpu.VMEM((SEQ, HEAD_DIM), bf),
            pltpu.VMEM((SEQ, 128), f32),
            pltpu.VMEM((3 * HEAD_DIM, SEQ), bf),
            pltpu.VMEM((SEQ, HEAD_DIM), f32),
            pltpu.VMEM((SEQ, HEAD_DIM), f32),
            pltpu.VMEM((D, SEQ), bf),
            pltpu.VMEM((PIX_PAD, 128), f32),
            pltpu.VMEM((D, PIX_PAD), f32),
            pltpu.VMEM((2, SEQ, QB), f32),
            pltpu.VMEM((2, SEQ, QB), f32),
            pltpu.VMEM((2, SEQ, QB), bf),
            pltpu.VMEM((2, SEQ, QB), bf),
            pltpu.VMEM((HALF // QB, D, QB), bf),
            pltpu.VMEM((2, D, QB), f32),
        ],
        compiler_params=pltpu.CompilerParams(vmem_limit_bytes=SCENE_VMEM),
    )(place, meta, *front, *loaded)


def exchange(x, axes):
    return lax.all_to_all(x, axes, 0, 0, tiled=True)


def shift_chips(x):
    return [lax.ppermute(x, "zi", [(i, (i + hop) % 3) for i in range(3)]) for hop in (1, 2)]


def swap_core(x):
    return lax.ppermute(x, "core", [(0, 1), (1, 0)])


def place_of(stored, zt, zi, core):
    owner, part = stored // 2, stored % 2
    chip, owner_core = owner // 2, owner % 2
    owner_t, owner_i = chip // 3, chip % 3
    inner = (zi - owner_i + 3) % 3
    block = jnp.where(owner_t == zt, 0, 6) + jnp.where(owner_core == core, 0, 3) + inner
    return (block * 2 + part).astype(jnp.int32)


def sum_over_z(column):
    parts = column.astype(jnp.bfloat16).reshape(2, 1, 6, PIX_PAD)
    parts = jnp.broadcast_to(parts, (2, 6, 6, PIX_PAD)).reshape(12, 6, PIX_PAD)
    own = jnp.sum(exchange(parts, ("zh", "zt", "zi")).astype(jnp.float32), axis=0)
    other = swap_core(own)
    first_core = lax.axis_index("core") == 0
    return jnp.concatenate(
        [jnp.where(first_core, own, other), jnp.where(first_core, other, own)], axis=0
    )


def per_device(
    tiles, tile_list, valid_tiles, patch_weight, norm_gain, norm_bias,
    w_query, w_key, w_value, w_out, cotangent,
):
    bf, f32 = jnp.bfloat16, jnp.float32
    position = lax.axis_index(SEQ_AXES)
    core = lax.axis_index("core")
    zt = lax.axis_index("zt")
    limit = valid_tiles[0] * TILE_TOK

    pixels = jnp.pad(tiles.reshape(TOK_DEV, PIX).T, ((0, PIX_ROW - PIX), (0, 0)))
    across = lax.ppermute(pixels, "zt", [(0, 1), (1, 0)])

    live_rows = position * TOK_DEV + jnp.arange(TOK_DEV) < limit
    cot_rows = cotangent[0]
    cot_live = jnp.where(live_rows[:, None], cot_rows, jnp.zeros_like(cot_rows))
    d_attn_t = dot(w_out, cot_live, 1, 1).astype(bf).reshape(HEADS, HEAD_DIM, TOK_DEV)
    start = position * HEAD_DIM
    parts = [lax.dynamic_slice_in_dim(w, start, HEAD_DIM, 1) for w in (w_query, w_key, w_value)]
    packed = jnp.concatenate([cot_live.T, *parts, jnp.zeros((D, HEAD_DIM), bf)], axis=1)
    weight = jnp.pad(patch_weight, ((0, 0), (0, PIX_PAD - PIX)))
    affine = jnp.broadcast_to(jnp.stack([norm_gain, norm_bias])[:, :, None], (2, D, 128))
    place = place_of(tile_list[0], zt, lax.axis_index("zi"), core)
    meta = jnp.stack([valid_tiles[0], position, core])

    near_own = jnp.stack([pixels, *shift_chips(pixels)])
    head_t = exchange(d_attn_t, SEQ_AXES)
    across, head_t, near_own, packed, weight, affine, place, meta = lax.optimization_barrier(
        (across, head_t, near_own, packed, weight, affine, place, meta)
    )
    shifted = shift_chips(across)
    near = (near_own, swap_core(near_own))
    front = embed_call(*near, weight, affine, packed)
    shifted, front = lax.optimization_barrier((shifted, front))
    far_own = jnp.stack([across, *shifted])
    far = (far_own, swap_core(far_own))
    keep, send = scene_call(
        place, meta, near, far, front, head_t, weight, packed, affine
    )

    got = swap_core(send)
    mine = (keep + got.astype(f32)).astype(bf)
    along_x = exchange(mine, "x")
    row_sum = jnp.sum(along_x.astype(f32), axis=0).astype(bf)
    along_y = exchange(row_sum.reshape(8, 12, PIX_PAD), "y")
    column = jnp.sum(along_y.astype(f32), axis=0)
    total = sum_over_z(column)[:, :PIX]
    return total * (float(64 * SEQ) ** (-0.5))


def solution(mesh):
    fine = Mesh(
        mesh.devices.reshape(8, 2, 4, 2, 3, 2), ("y", "zh", "x", "zt", "zi", "core")
    )
    in_specs = (
        P(DP_AXES, SEQ_AXES, None, None), P(DP_AXES, None), P(DP_AXES),
        P(), P(), P(), P(), P(), P(), P(), P(DP_AXES, SEQ_AXES, None),
    )
    return jax.shard_map(
        per_device, mesh=fine, in_specs=in_specs, out_specs=P(DP_AXES, None), check_vma=False
    )
```

time: 172 us -> 140 us (0.81)
  waiting for transfers between devices: 42.8 us -> 10.4 us
  starting transfers between devices: 25.8 us -> 43.7 us
  blocking collectives: 62.1 us -> 46 us
  Pallas kernels: 29.7 us -> 23.7 us
  local copies, waits for them, and re-layouts: 7.12 us -> 10.8 us
    all_to_all x1 -> x0, waiting for transfers between devices: 29.9 us -> none  [gather(): return lax.all_to_all(copies, axes, 0, 0, tiled=False)]
    ppermute x1 -> x9, starting transfers between devices: 7.62 us -> 36.2 us  [the longest x4 13.8 us: shift_chips(): lax.ppermute(x, 'zi', [(i, (i + hop) % 3) for i in range(3)])]
    all_to_all x2 -> x0, blocking collectives: 27 us -> none  [gather(): return lax.all_to_all(copies, axes, 0, 0, tiled=False)]
    all_to_all x3, blocking collectives: 35.1 us -> 46 us  [exchange(): return lax.all_to_all(x, axes, 0, 0, tiled=True)]
    all_to_all x1, waiting for transfers between devices: 12 us -> 3.89 us  [exchange(): return lax.all_to_all(x, axes, 0, 0, tiled=True)]
    all_to_all x1, starting transfers between devices: 13.9 us -> 7.51 us  [exchange(): return lax.all_to_all(x, axes, 0, 0, tiled=True)]
    pallas_call x1 -> x2, Pallas kernels: 29.7 us -> 23.7 us  [the longest x1 20.6 us: scene_call(): pl.pallas_call(scene_kernel, out_shape=(jax.ShapeDtypeStruct((4, 96, PIX_...]
    ppermute x1 -> x9, waiting for transfers between devices: 0.84 us -> 6.48 us  [the longest x4 3.71 us: swap_core(): return lax.ppermute(x, 'core', [(0, 1), (1, 0)])]
  transfers between devices with their start and end apart: 3 -> 10, of which waited for: 3 -> 5; matrix products, arithmetic and copies ran while one was open for 2% -> 7% of each run, Pallas kernels for 0% -> 2%
where the time goes in v2:
time: 140 us; the launch traced here: 139 us
  blocking collectives  46 us (33%)
  starting transfers between devices  43.7 us (31%)
  Pallas kernels  23.7 us (17%)
  local copies, waits for them, and re-layouts  10.8 us (8%)
  waiting for transfers between devices  10.4 us (7%)
  other arithmetic  3.13 us (2%)
    all_to_all x3, blocking collectives, exchange(): return lax.all_to_all(x, axes, 0, 0, tiled=True)  46 us
    pallas_call x1, Pallas kernels, scene_call(): pl.pallas_call(scene_kernel, out_shape=(jax.ShapeDtypeStruct((4, 96, PIX_...  20.6 us
    ppermute x4, starting transfers between devices, shift_chips(): lax.ppermute(x, 'zi', [(i, (i + hop) % 3) for i in range(3)])  13.8 us
    ppermute x4, starting transfers between devices, swap_core(): return lax.ppermute(x, 'core', [(0, 1), (1, 0)])  13.5 us
    ppermute x1, starting transfers between devices, per_device(): across = lax.ppermute(pixels, 'zt', [(0, 1), (1, 0)])  8.83 us
    all_to_all x1, starting transfers between devices, exchange(): return lax.all_to_all(x, axes, 0, 0, tiled=True)  7.51 us
    all_to_all x1, waiting for transfers between devices, exchange(): return lax.all_to_all(x, axes, 0, 0, tiled=True)  3.89 us
    ppermute x4, waiting for transfers between devices, swap_core(): return lax.ppermute(x, 'core', [(0, 1), (1, 0)])  3.71 us
  transfers between devices with their start and end apart: 10, of which 5 were waited for; matrix products, arithmetic and copies ran while one was open for 7% of the time, Pallas kernels for 2%

profile of v2, /device:TPU:1, one launch (start us, length us, event | category | flops | bytes accessed | tf_op | source)
XLA Modules:
  0.0 139.2 jit_solution(17684723515213306837)
XLA Ops:
  0.0 1.2 copy.20
  1.2 0.8 pad_bitcast_fusion
  1.9 4.8 %collective-permute-start.1 = (bf16[592,128]{1,0:T(8,128)(2,1)}, bf16[592,128]{1,0:T(8,128)(2,1)}, u32[]{:S(2)}, u32[]{:S(2)}) collective-permute-start(bf16[592,128]{1,0:T(8,128)(2,1)} %get-tuple-element.42), channel_id=1, source_target_pairs={{0,2},{2,4},{4,0},{1,3},{3,5},{5,1},{6,8},{8,10},{10,6},{7,9},{9,1... | collective-permute-start | bytes 454664 | tf_op jit(solution)/shard_map/ppermute | solution.py:345
  6.7 3.7 %collective-permute-start.2 = (bf16[592,128]{1,0:T(8,128)(2,1)}, bf16[592,128]{1,0:T(8,128)(2,1)}, u32[]{:S(2)}, u32[]{:S(2)}) collective-permute-start(bf16[592,128]{1,0:T(8,128)(2,1)} %get-tuple-element.42), channel_id=1, source_target_pairs={{0,4},{2,0},{4,2},{1,5},{3,1},{5,3},{6,10},{8,6},{10,8},{7,11},{9,... | collective-permute-start | bytes 454664 | tf_op jit(solution)/shard_map/ppermute | solution.py:345
  10.5 8.8 %collective-permute-start = (bf16[592,128]{1,0:T(8,128)(2,1)}, bf16[592,128]{1,0:T(8,128)(2,1)}, u32[]{:S(2)}, u32[]{:S(2)}) collective-permute-start(bf16[592,128]{1,0:T(8,128)(2,1)} %get-tuple-element.42), channel_id=1, source_target_pairs={{0,6},{6,0},{1,7},{7,1},{2,8},{8,2},{3,9},{9,3},{4,10},{10,4},{5,1... | collective-permute-start | bytes 454664 | tf_op jit(solution)/shard_map/ppermute | solution.py:383
  20.0 1.1 copy.21
  21.1 0.5 fusion
  21.7 0.8 copy.22
  22.5 7.5 %all-to-all-start = ((bf16[12,64,128]{2,1,0:T(8,128)(2,1)}), bf16[12,64,128]{2,1,0:T(8,128)(2,1)S(1)}, u32[]{:S(2)}, u32[]{:S(2)}) async-start(bf16[12,64,128]{2,1,0:T(8,128)(2,1)} %bitcast.5), calls=%async_computation | async-start | bytes 393216 | tf_op jit(solution)/shard_map/all_to_all | solution.py:341
  30.1 1.7 %constant_dynamic-slice_fusion.2 = bf16[768,64]{1,0:T(8,128)(2,1)} fusion(bf16[768,768]{1,0:T(8,128)(2,1)} %param.17, s32[]{:T(128)S(6)} %select_n.60), kind=kLoop, calls=%fused_computation.31 | loop fusion | bytes 196612 | tf_op jit(solution)/shard_map/dynamic_slice | solution.py:390
  31.8 1.9 %constant_dynamic-slice_fusion = (bf16[768,64]{1,0:T(8,128)(2,1)}, bf16[768,64]{1,0:T(8,128)(2,1)}) fusion(bf16[768,768]{1,0:T(8,128)(2,1)} %param.19, s32[]{:T(128)S(6)} %select_n.60, bf16[768,768]{1,0:T(8,128)(2,1)} %param.18), kind=kLoop, calls=%fused_computation.29 | loop fusion | bytes 393220 | tf_op jit(solution)/shard_map/dynamic_slice | solution.py:390
  33.9 1.5 %copy.23 = bf16[768,588]{1,0:T(8,128)(2,1)S(1)} copy(bf16[768,588]{0,1:T(8,128)(2,1)} %param.14) | data formatting | bytes 1806336 | tf_op args[3]
  35.6 1.4 concatenate.6.pack_hbm
  37.0 1.1 pad_maximum_fusion.own_hbm.near_own_hbm
  38.1 3.9 %all-to-all-done.head_hbm = bf16[12,64,128]{2,1,0:T(8,128)(2,1)S(1)} async-done(((bf16[12,64,128]{2,1,0:T(8,128)(2,1)}), bf16[12,64,128]{2,1,0:T(8,128)(2,1)S(1)}, u32[]{:S(2)}, u32[]{:S(2)}) %all-to-all-start) | async-done | bytes 196640 | tf_op jit(solution)/shard_map/all_to_all | solution.py:341
  42.2 2.3 %collective-permute-start.5 = (bf16[3,592,128]{2,1,0:T(8,128)(2,1)S(1)}, bf16[3,592,128]{2,1,0:T(8,128)(2,1)S(1)}, u32[]{:S(2)}, u32[]{:S(2)}) collective-permute-start(bf16[3,592,128]{2,1,0:T(8,128)(2,1)S(1)} %pad_maximum_fusion.own_hbm.near_own_hbm), channel_id=1, source_target_pairs={{0,1},{1,0},{2,3},{3,2},{4,5},{5,4},{6,7},{7,6},{8,9},{9,8},{10,11... | collective-permute-start | bytes 1363976 | tf_op jit(solution)/shard_map/ppermute | solution.py:349
  44.6 1.9 %collective-permute-start.4 = (bf16[592,128]{1,0:T(8,128)(2,1)}, bf16[592,128]{1,0:T(8,128)(2,1)S(1)}, u32[]{:S(2)}, u32[]{:S(2)}) collective-permute-start(bf16[592,128]{1,0:T(8,128)(2,1)} %collective-permute-done), channel_id=1, source_target_pairs={{0,4},{2,0},{4,2},{1,5},{3,1},{5,3},{6,10},{8,6},{10,8},{7,11},{9,... | collective-permute-start | bytes 454664 | tf_op jit(solution)/shard_map/ppermute | solution.py:345
  46.5 3.4 %collective-permute-start.3 = (bf16[592,128]{1,0:T(8,128)(2,1)}, bf16[592,128]{1,0:T(8,128)(2,1)S(1)}, u32[]{:S(2)}, u32[]{:S(2)}) collective-permute-start(bf16[592,128]{1,0:T(8,128)(2,1)} %collective-permute-done), channel_id=1, source_target_pairs={{0,2},{2,4},{4,0},{1,3},{3,5},{5,1},{6,8},{8,10},{10,6},{7,9},{9,1... | collective-permute-start | bytes 454664 | tf_op jit(solution)/shard_map/ppermute | solution.py:345
  49.9 3.1 %shard_map.109 = (f32[1,768]{1,0:T(1,128)S(1)}, f32[1,768]{1,0:T(1,128)S(1)}, bf16[192,768]{1,0:T(8,128)(2,1)S(1)}) custom-call(bf16[3,592,128]{2,1,0:T(8,128)(2,1)S(1)} %pad_maximum_fusion.own_hbm.near_own_hbm, bf16[3,592,128]{2,1,0:T(8,128)(2,1)S(1)} %collective-permute-done.5.other_hbm.near_other_hbm, bf16[768,640]{1,0:T(8,128)(2,1)S(1)} %pad.9.weight_hbm, ...), custom_call_target="tpu_custom_call" | custom-call | tf_op jit(solution)/shard_map/pallas_call | solution.py:110
  53.0 2.8 %collective-permute-done.3 = bf16[592,128]{1,0:T(8,128)(2,1)S(1)} collective-permute-done((bf16[592,128]{1,0:T(8,128)(2,1)}, bf16[592,128]{1,0:T(8,128)(2,1)S(1)}, u32[]{:S(2)}, u32[]{:S(2)}) %collective-permute-start.3) | collective-permute-done | bytes 151584 | tf_op jit(solution)/shard_map/ppermute | solution.py:345
  55.7 1.0 pad_maximum_fusion.1.far_own_hbm
  56.7 2.8 %collective-permute-start.6 = (bf16[3,592,128]{2,1,0:T(8,128)(2,1)S(1)}, bf16[3,592,128]{2,1,0:T(8,128)(2,1)S(1)}, u32[]{:S(2)}, u32[]{:S(2)}) collective-permute-start(bf16[3,592,128]{2,1,0:T(8,128)(2,1)S(1)} %pad_maximum_fusion.1.far_own_hbm), channel_id=1, source_target_pairs={{0,1},{1,0},{2,3},{3,2},{4,5},{5,4},{6,7},{7,6},{8,9},{9,8},{10,11... | collective-permute-start | bytes 1363976 | tf_op jit(solution)/shard_map/ppermute | solution.py:349
  59.5 1.4 %collective-permute-done.6.far_other_hbm = bf16[3,592,128]{2,1,0:T(8,128)(2,1)S(1)} collective-permute-done((bf16[3,592,128]{2,1,0:T(8,128)(2,1)S(1)}, bf16[3,592,128]{2,1,0:T(8,128)(2,1)S(1)}, u32[]{:S(2)}, u32[]{:S(2)}) %collective-permute-start.6) | collective-permute-done | bytes 454688 | tf_op jit(solution)/shard_map/ppermute | solution.py:349
  60.9 20.6 %shard_map.110 = (f32[4,96,640]{2,1,0:T(8,128)S(1)}, bf16[4,96,640]{2,1,0:T(8,128)(2,1)S(1)}) custom-call(s32[24]{0:T(128)S(1)} %fusion.5.place_ref, s32[3]{0:T(128)S(1)} %pad_add_fusion.meta_ref, f32[1,768]{1,0:T(1,128)S(1)} %get-tuple-element.33.mean_a, f32[1,768]{1,0:T(1,128)S(1)} %get-tuple-element.34.istd_a, ...), custom_call_target="tpu_custom_call" | custom-call | tf_op jit(solution)/shard_map/pallas_call | solution.py:299
  81.5 2.3 %collective-permute-start.7 = (bf16[4,96,640]{2,1,0:T(8,128)(2,1)S(1)}, bf16[4,96,640]{2,1,0:T(8,128)(2,1)S(1)}, u32[]{:S(2)}, u32[]{:S(2)}) collective-permute-start(bf16[4,96,640]{2,1,0:T(8,128)(2,1)S(1)} %get-tuple-element.40), channel_id=1, source_target_pairs={{0,1},{1,0},{2,3},{3,2},{4,5},{5,4},{6,7},{7,6},{8,9},{9,8},{10,11... | collective-permute-start | bytes 1474568 | tf_op jit(solution)/shard_map/ppermute | solution.py:349
  83.8 1.5 %collective-permute-done.7 = bf16[4,96,640]{2,1,0:T(8,128)(2,1)S(1)} collective-permute-done((bf16[4,96,640]{2,1,0:T(8,128)(2,1)S(1)}, bf16[4,96,640]{2,1,0:T(8,128)(2,1)S(1)}, u32[]{:S(2)}, u32[]{:S(2)}) %collective-permute-start.7) | collective-permute-done | bytes 491552 | tf_op jit(solution)/shard_map/ppermute | solution.py:349
  85.4 11.2 %all_to_all.20 = bf16[4,96,640]{2,1,0:T(8,128)(2,1)S(1)} all-to-all(bf16[4,96,640]{2,1,0:T(8,128)(2,1)S(1)} %add_convert_fusion), channel_id=1, replica_groups=mesh['y'=8,'zh'=2,'x'=4,'zt'=2,'zi'=3,'core'=2] {'x'}, dimensions={0} | all-to-all | bytes 983040 | tf_op jit(solution)/shard_map/all_to_all | solution.py:341
  96.8 13.0 %all_to_all.21 = bf16[8,12,640]{2,1,0:T(8,128)(2,1)S(1)} all-to-all(bf16[8,12,640]{2,1,0:T(8,128)(2,1)S(1)} %reshape.24), channel_id=1, replica_groups=mesh['y'=8,'zh'=2,'x'=4,'zt'=2,'zi'=3,'core'=2] {'y'}, dimensions={0} | all-to-all | bytes 245760 | tf_op jit(solution)/shard_map/all_to_all | solution.py:341
  109.8 21.8 %all_to_all.22 = bf16[12,6,640]{2,1,0:T(8,128)(2,1)S(1)} all-to-all(bf16[12,6,640]{2,1,0:T(8,128)(2,1)S(1)} %bitcast.38), channel_id=1, replica_groups=mesh['y'=8,'zh'=2,'x'=4,'zt'=2,'zi'=3,'core'=2] {'zh','zt','zi'}, dimensions={0} | all-to-all | bytes 184320 | tf_op jit(solution)/shard_map/all_to_all | solution.py:341
  131.6 6.1 %collective-permute-start.8 = (f32[6,640]{1,0:T(8,128)S(1)}, f32[6,640]{1,0:T(8,128)S(1)}, u32[]{:S(2)}, u32[]{:S(2)}) collective-permute-start(f32[6,640]{1,0:T(8,128)S(1)} %convert_reduce_fusion), channel_id=1, source_target_pairs={{0,1},{1,0},{2,3},{3,2},{4,5},{5,4},{6,7},{7,6},{8,9},{9,8},{10,11... | collective-permute-start | bytes 46088 | tf_op jit(solution)/shard_map/ppermute | solution.py:349
  137.8 0.8 collective-permute-done.8
  138.6 0.6 fusion.3
  (31 shorter events, 0.9 us)
Async XLA Ops:
  0.0 21.1 %copy-start = (bf16[768,768]{1,0:T(8,128)(2,1)S(1)}, bf16[768,768]{1,0:T(8,128)(2,1)}, u32[]{:S(2)}) copy-start(bf16[768,768]{1,0:T(8,128)(2,1)} %param.20) | copy-start | bytes 3538948
  1.9 35.0 %collective-permute-start.1 = (bf16[592,128]{1,0:T(8,128)(2,1)}, bf16[592,128]{1,0:T(8,128)(2,1)}, u32[]{:S(2)}, u32[]{:S(2)}) collective-permute-start(bf16[592,128]{1,0:T(8,128)(2,1)} %get-tuple-element.42), channel_id=1, source_target_pairs={{0,2},{2,4},{4,0},{1,3},{3,5},{5,1},{6,8},{8,10},{10,6},{7,9},{9,1... | collective-permute-start | bytes 454664 | tf_op jit(solution)/shard_map/ppermute | solution.py:345
  6.7 30.2 %collective-permute-start.2 = (bf16[592,128]{1,0:T(8,128)(2,1)}, bf16[592,128]{1,0:T(8,128)(2,1)}, u32[]{:S(2)}, u32[]{:S(2)}) collective-permute-start(bf16[592,128]{1,0:T(8,128)(2,1)} %get-tuple-element.42), channel_id=1, source_target_pairs={{0,4},{2,0},{4,2},{1,5},{3,1},{5,3},{6,10},{8,6},{10,8},{7,11},{9,... | collective-permute-start | bytes 454664 | tf_op jit(solution)/shard_map/ppermute | solution.py:345
  10.5 27.6 %collective-permute-start = (bf16[592,128]{1,0:T(8,128)(2,1)}, bf16[592,128]{1,0:T(8,128)(2,1)}, u32[]{:S(2)}, u32[]{:S(2)}) collective-permute-start(bf16[592,128]{1,0:T(8,128)(2,1)} %get-tuple-element.42), channel_id=1, source_target_pairs={{0,6},{6,0},{1,7},{7,1},{2,8},{8,2},{3,9},{9,3},{4,10},{10,4},{5,1... | collective-permute-start | bytes 454664 | tf_op jit(solution)/shard_map/ppermute | solution.py:383
  21.1 8.9 %copy-start.1 = (f32[768]{0:T(1024)S(1)}, f32[768]{0:T(1024)}, u32[]{:S(2)}) copy-start(f32[768]{0:T(1024)} %param.15) | copy-start | bytes 9220
  21.1 8.9 %copy-start.2 = (f32[768]{0:T(1024)S(1)}, f32[768]{0:T(1024)}, u32[]{:S(2)}) copy-start(f32[768]{0:T(1024)} %param.16) | copy-start | bytes 9220
  21.7 12.1 %copy-start.3 = (s32[1,24]{1,0:T(1,128)S(1)}, s32[1,24]{1,0:T(1,128)}, u32[]{:S(2)}) copy-start(s32[1,24]{1,0:T(1,128)} %param.12) | copy-start | bytes 292
  22.5 19.5 %all-to-all-start = ((bf16[12,64,128]{2,1,0:T(8,128)(2,1)}), bf16[12,64,128]{2,1,0:T(8,128)(2,1)S(1)}, u32[]{:S(2)}, u32[]{:S(2)}) async-start(bf16[12,64,128]{2,1,0:T(8,128)(2,1)} %bitcast.5), calls=%async_computation | async-start | bytes 393216 | tf_op jit(solution)/shard_map/all_to_all | solution.py:341
  42.2 7.6 %collective-permute-start.5 = (bf16[3,592,128]{2,1,0:T(8,128)(2,1)S(1)}, bf16[3,592,128]{2,1,0:T(8,128)(2,1)S(1)}, u32[]{:S(2)}, u32[]{:S(2)}) collective-permute-start(bf16[3,592,128]{2,1,0:T(8,128)(2,1)S(1)} %pad_maximum_fusion.own_hbm.near_own_hbm), channel_id=1, source_target_pairs={{0,1},{1,0},{2,3},{3,2},{4,5},{5,4},{6,7},{7,6},{8,9},{9,8},{10,11... | collective-permute-start | bytes 1363976 | tf_op jit(solution)/shard_map/ppermute | solution.py:349
  44.6 8.4 %collective-permute-start.4 = (bf16[592,128]{1,0:T(8,128)(2,1)}, bf16[592,128]{1,0:T(8,128)(2,1)S(1)}, u32[]{:S(2)}, u32[]{:S(2)}) collective-permute-start(bf16[592,128]{1,0:T(8,128)(2,1)} %collective-permute-done), channel_id=1, source_target_pairs={{0,4},{2,0},{4,2},{1,5},{3,1},{5,3},{6,10},{8,6},{10,8},{7,11},{9,... | collective-permute-start | bytes 454664 | tf_op jit(solution)/shard_map/ppermute | solution.py:345
  46.5 9.3 %collective-permute-start.3 = (bf16[592,128]{1,0:T(8,128)(2,1)}, bf16[592,128]{1,0:T(8,128)(2,1)S(1)}, u32[]{:S(2)}, u32[]{:S(2)}) collective-permute-start(bf16[592,128]{1,0:T(8,128)(2,1)} %collective-permute-done), channel_id=1, source_target_pairs={{0,2},{2,4},{4,0},{1,3},{3,5},{5,1},{6,8},{8,10},{10,6},{7,9},{9,1... | collective-permute-start | bytes 454664 | tf_op jit(solution)/shard_map/ppermute | solution.py:345
  56.7 4.2 %collective-permute-start.6 = (bf16[3,592,128]{2,1,0:T(8,128)(2,1)S(1)}, bf16[3,592,128]{2,1,0:T(8,128)(2,1)S(1)}, u32[]{:S(2)}, u32[]{:S(2)}) collective-permute-start(bf16[3,592,128]{2,1,0:T(8,128)(2,1)S(1)} %pad_maximum_fusion.1.far_own_hbm), channel_id=1, source_target_pairs={{0,1},{1,0},{2,3},{3,2},{4,5},{5,4},{6,7},{7,6},{8,9},{9,8},{10,11... | collective-permute-start | bytes 1363976 | tf_op jit(solution)/shard_map/ppermute | solution.py:349
  81.5 3.8 %collective-permute-start.7 = (bf16[4,96,640]{2,1,0:T(8,128)(2,1)S(1)}, bf16[4,96,640]{2,1,0:T(8,128)(2,1)S(1)}, u32[]{:S(2)}, u32[]{:S(2)}) collective-permute-start(bf16[4,96,640]{2,1,0:T(8,128)(2,1)S(1)} %get-tuple-element.40), channel_id=1, source_target_pairs={{0,1},{1,0},{2,3},{3,2},{4,5},{5,4},{6,7},{7,6},{8,9},{9,8},{10,11... | collective-permute-start | bytes 1474568 | tf_op jit(solution)/shard_map/ppermute | solution.py:349
  131.6 7.0 %collective-permute-start.8 = (f32[6,640]{1,0:T(8,128)S(1)}, f32[6,640]{1,0:T(8,128)S(1)}, u32[]{:S(2)}, u32[]{:S(2)}) collective-permute-start(f32[6,640]{1,0:T(8,128)S(1)} %convert_reduce_fusion), channel_id=1, source_target_pairs={{0,1},{1,0},{2,3},{3,2},{4,5},{5,4},{6,7},{7,6},{8,9},{9,8},{10,11... | collective-permute-start | bytes 46088 | tf_op jit(solution)/shard_map/ppermute | solution.py:349

commit v3 on v2

--- a/solution.py
+++ b/solution.py
@@ -23,7 +23,6 @@
 SCENE_VMEM = 38 << 20
 
 DP_AXES = ("y", "zh", "x")
-CHIP_AXES = ("zt", "zi")
 SEQ_AXES = ("zt", "zi", "core")
 
 
@@ -381,6 +380,7 @@
 
     pixels = jnp.pad(tiles.reshape(TOK_DEV, PIX).T, ((0, PIX_ROW - PIX), (0, 0)))
     across = lax.ppermute(pixels, "zt", [(0, 1), (1, 0)])
+    near_shifts = shift_chips(pixels)
 
     live_rows = position * TOK_DEV + jnp.arange(TOK_DEV) < limit
     cot_rows = cotangent[0]
@@ -394,13 +394,12 @@
     place = place_of(tile_list[0], zt, lax.axis_index("zi"), core)
     meta = jnp.stack([valid_tiles[0], position, core])
 
-    near_own = jnp.stack([pixels, *shift_chips(pixels)])
     head_t = exchange(d_attn_t, SEQ_AXES)
-    across, head_t, near_own, packed, weight, affine, place, meta = lax.optimization_barrier(
-        (across, head_t, near_own, packed, weight, affine, place, meta)
-    )
+    near_own = jnp.stack([pixels, *near_shifts])
+    across, near_own = lax.optimization_barrier((across, near_own))
     shifted = shift_chips(across)
     near = (near_own, swap_core(near_own))
+    packed, weight, affine, near = lax.optimization_barrier((packed, weight, affine, near))
     front = embed_call(*near, weight, affine, packed)
     shifted, front = lax.optimization_barrier((shifted, front))
     far_own = jnp.stack([across, *shifted])
@@ -427,6 +426,7 @@
         P(DP_AXES, SEQ_AXES, None, None), P(DP_AXES, None), P(DP_AXES),
         P(), P(), P(), P(), P(), P(), P(), P(DP_AXES, SEQ_AXES, None),
     )
+
     return jax.shard_map(
         per_device, mesh=fine, in_specs=in_specs, out_specs=P(DP_AXES, None), check_vma=False
     )

time: 140 us -> 139 us (level)
  waiting for transfers between devices: 10.4 us -> 3.93 us
  local copies, waits for them, and re-layouts: 10.8 us -> 15.7 us
    all_to_all x1, waiting for transfers between devices: 3.89 us -> 0.01 us  [exchange(): return lax.all_to_all(x, axes, 0, 0, tiled=True)]
    unnamed x10 -> x22, local copies, waits for them, and re-layouts: 2.65 us -> 6.14 us
    ppermute x4, waiting for transfers between devices: 2.77 us -> 0.01 us  [shift_chips(): lax.ppermute(x, 'zi', [(i, (i + hop) % 3) for i in range(3)])]
    all_to_all x3, blocking collectives: 46 us -> 47.4 us  [exchange(): return lax.all_to_all(x, axes, 0, 0, tiled=True)]
  transfers between devices with their start and end apart: 10 -> 10, of which waited for: 5 -> 3; matrix products, arithmetic and copies ran while one was open for 7% -> 10% of each run, Pallas kernels for 2% -> 2%
where the time goes in v3:
time: 139 us
  blocking collectives  47.4 us (34%)
  starting transfers between devices  44 us (32%)
  Pallas kernels  23.1 us (17%)
  local copies, waits for them, and re-layouts  15.7 us (11%)
  waiting for transfers between devices  3.93 us (3%)
  other arithmetic  2.95 us (2%)
    all_to_all x3, blocking collectives, exchange(): return lax.all_to_all(x, axes, 0, 0, tiled=True)  47.4 us
    pallas_call x1, Pallas kernels, scene_call(): pl.pallas_call(scene_kernel, out_shape=(jax.ShapeDtypeStruct((4, 96, PIX_...  19.8 us
    ppermute x4, starting transfers between devices, shift_chips(): lax.ppermute(x, 'zi', [(i, (i + hop) % 3) for i in range(3)])  14.9 us
    ppermute x4, starting transfers between devices, swap_core(): return lax.ppermute(x, 'core', [(0, 1), (1, 0)])  12.7 us
    ppermute x1, starting transfers between devices, per_device(): across = lax.ppermute(pixels, 'zt', [(0, 1), (1, 0)])  8.83 us
    all_to_all x1, starting transfers between devices, exchange(): return lax.all_to_all(x, axes, 0, 0, tiled=True)  7.51 us
    unnamed x22, local copies, waits for them, and re-layouts  6.14 us
    ppermute x4, waiting for transfers between devices, swap_core(): return lax.ppermute(x, 'core', [(0, 1), (1, 0)])  3.91 us
  transfers between devices with their start and end apart: 10, of which 3 were waited for; matrix products, arithmetic and copies ran while one was open for 10% of the time, Pallas kernels for 2%

profile of v3, /device:TPU:1, one launch (start us, length us, event | category | flops | bytes accessed | tf_op | source)
XLA Modules:
  0.0 138.6 jit_solution(17304308426207980077)
XLA Ops:
  0.0 1.2 copy.20
  1.2 4.8 %collective-permute-start.1 = (bf16[592,128]{1,0:T(8,128)(2,1)S(1)}, bf16[592,128]{1,0:T(8,128)(2,1)S(1)}, u32[]{:S(2)}, u32[]{:S(2)}) collective-permute-start(bf16[592,128]{1,0:T(8,128)(2,1)S(1)} %get-tuple-element.40), channel_id=1, source_target_pairs={{0,2},{2,4},{4,0},{1,3},{3,5},{5,1},{6,8},{8,10},{10,6},{7,9},{9,1... | collective-permute-start | bytes 454664 | tf_op jit(solution)/shard_map/ppermute | solution.py:344
  6.0 3.7 %collective-permute-start.2 = (bf16[592,128]{1,0:T(8,128)(2,1)S(1)}, bf16[592,128]{1,0:T(8,128)(2,1)S(1)}, u32[]{:S(2)}, u32[]{:S(2)}) collective-permute-start(bf16[592,128]{1,0:T(8,128)(2,1)S(1)} %get-tuple-element.40), channel_id=1, source_target_pairs={{0,4},{2,0},{4,2},{1,5},{3,1},{5,3},{6,10},{8,6},{10,8},{7,11},{9,... | collective-permute-start | bytes 454664 | tf_op jit(solution)/shard_map/ppermute | solution.py:344
  9.8 8.8 %collective-permute-start = (bf16[592,128]{1,0:T(8,128)(2,1)S(1)}, bf16[592,128]{1,0:T(8,128)(2,1)}, u32[]{:S(2)}, u32[]{:S(2)}) collective-permute-start(bf16[592,128]{1,0:T(8,128)(2,1)S(1)} %get-tuple-element.40), channel_id=1, source_target_pairs={{0,6},{6,0},{1,7},{7,1},{2,8},{8,2},{3,9},{9,3},{4,10},{10,4},{5,1... | collective-permute-start | bytes 454664 | tf_op jit(solution)/shard_map/ppermute | solution.py:382
  19.3 1.1 copy.21
  20.9 0.8 copy.23
  21.8 7.5 %all-to-all-start = ((bf16[12,64,128]{2,1,0:T(8,128)(2,1)}), bf16[12,64,128]{2,1,0:T(8,128)(2,1)}, u32[]{:S(2)}, u32[]{:S(2)}) async-start(bf16[12,64,128]{2,1,0:T(8,128)(2,1)} %bitcast.15), calls=%async_computation | async-start | bytes 393216 | tf_op jit(solution)/shard_map/all_to_all | solution.py:340
  29.3 2.0 %constant_dynamic-slice_fusion = (bf16[768,64]{1,0:T(8,128)(2,1)}, bf16[768,64]{1,0:T(8,128)(2,1)}) fusion(bf16[768,768]{1,0:T(8,128)(2,1)} %param.19, s32[]{:T(128)S(6)} %select_n.69, bf16[768,768]{1,0:T(8,128)(2,1)} %param.18), kind=kLoop, calls=%fused_computation.29 | loop fusion | bytes 393220 | tf_op jit(solution)/shard_map/dynamic_slice | solution.py:390
  31.4 2.0 %collective-permute-start.5 = (bf16[3,592,128]{2,1,0:T(8,128)(2,1)S(1)}, bf16[3,592,128]{2,1,0:T(8,128)(2,1)}, u32[]{:S(2)}, u32[]{:S(2)}) collective-permute-start(bf16[3,592,128]{2,1,0:T(8,128)(2,1)S(1)} %pad_maximum_fusion.own_hbm.near_own_hbm), channel_id=1, source_target_pairs={{0,1},{1,0},{2,3},{3,2},{4,5},{5,4},{6,7},{7,6},{8,9},{9,8},{10,11... | collective-permute-start | bytes 1363976 | tf_op jit(solution)/shard_map/ppermute | solution.py:348
  33.4 4.5 %collective-permute-start.4 = (bf16[592,128]{1,0:T(8,128)(2,1)}, bf16[592,128]{1,0:T(8,128)(2,1)}, u32[]{:S(2)}, u32[]{:S(2)}) collective-permute-start(bf16[592,128]{1,0:T(8,128)(2,1)} %collective-permute-done), channel_id=1, source_target_pairs={{0,4},{2,0},{4,2},{1,5},{3,1},{5,3},{6,10},{8,6},{10,8},{7,11},{9,... | collective-permute-start | bytes 454664 | tf_op jit(solution)/shard_map/ppermute | solution.py:344
  37.9 1.9 %collective-permute-start.3 = (bf16[592,128]{1,0:T(8,128)(2,1)}, bf16[592,128]{1,0:T(8,128)(2,1)}, u32[]{:S(2)}, u32[]{:S(2)}) collective-permute-start(bf16[592,128]{1,0:T(8,128)(2,1)} %collective-permute-done), channel_id=1, source_target_pairs={{0,2},{2,4},{4,0},{1,3},{3,5},{5,1},{6,8},{8,10},{10,6},{7,9},{9,1... | collective-permute-start | bytes 454664 | tf_op jit(solution)/shard_map/ppermute | solution.py:344
  39.9 1.7 %constant_dynamic-slice_fusion.2 = bf16[768,64]{1,0:T(8,128)(2,1)} fusion(bf16[768,768]{1,0:T(8,128)(2,1)} %param.17, s32[]{:T(128)S(6)} %select_n.69), kind=kLoop, calls=%fused_computation.31 | loop fusion | bytes 196612 | tf_op jit(solution)/shard_map/dynamic_slice | solution.py:390
  41.6 1.3 copy.22
  42.9 1.3 pad.9.weight_hbm
  44.2 0.7 broadcast_in_dim.39
  45.0 1.4 %concatenate.6.pack_hbm = bf16[768,384]{1,0:T(8,128)(2,1)S(1)} concatenate(bf16[768,128]{1,0:T(8,128)(2,1)S(1)} %fusion.1, bf16[768,64]{1,0:T(8,128)(2,1)} %constant_dynamic-slice_fusion.2, bf16[768,64]{1,0:T(8,128)(2,1)} %get-tuple-element.44, bf16[768,64]{1,0:T(8,128)(2,1)} %get-tuple-element.43, bf16[768,64]{1,0:T(8,128)(2,1)} %broadcast_in_dim.39), dimensions={1} | concatenate | bytes 1179648 | tf_op jit(solution)/shard_map/concatenate | solution.py:391
  46.7 1.0 copy-done.2
  47.7 3.4 %shard_map.109 = (f32[1,768]{1,0:T(1,128)S(1)}, f32[1,768]{1,0:T(1,128)S(1)}, bf16[192,768]{1,0:T(8,128)(2,1)S(1)}) custom-call(bf16[3,592,128]{2,1,0:T(8,128)(2,1)S(1)} %copy-done.2, bf16[3,592,128]{2,1,0:T(8,128)(2,1)} %collective-permute-done.5.other_hbm.near_other_hbm, bf16[768,640]{1,0:T(8,128)(2,1)S(1)} %pad.9.weight_hbm, ...), custom_call_target="tpu_custom_call" | custom-call | tf_op jit(solution)/shard_map/pallas_call | solution.py:109
  51.1 0.7 copy-done.4
  51.8 1.9 %pad_maximum_fusion.1.far_own_hbm = bf16[3,592,128]{2,1,0:T(8,128)(2,1)} fusion(bf16[1,592,128]{2,1,0:T(8,128)(2,1)} %bitcast.13, bf16[1,592,128]{2,1,0:T(8,128)(2,1)} %bitcast.12, bf16[1,592,128]{2,1,0:T(8,128)(2,1)} %bitcast.11), kind=kLoop, calls=%fused_computation.4 | loop fusion | flops 454656 | bytes 909312 | tf_op jit(solution)/shard_map/stack | solution.py:405
  53.6 2.3 %collective-permute-start.6 = (bf16[3,592,128]{2,1,0:T(8,128)(2,1)}, bf16[3,592,128]{2,1,0:T(8,128)(2,1)}, u32[]{:S(2)}, u32[]{:S(2)}) collective-permute-start(bf16[3,592,128]{2,1,0:T(8,128)(2,1)} %pad_maximum_fusion.1.far_own_hbm), channel_id=1, source_target_pairs={{0,1},{1,0},{2,3},{3,2},{4,5},{5,4},{6,7},{7,6},{8,9},{9,8},{10,11... | collective-permute-start | bytes 1363976 | tf_op jit(solution)/shard_map/ppermute | solution.py:348
  56.1 1.6 %collective-permute-done.6.far_other_hbm = bf16[3,592,128]{2,1,0:T(8,128)(2,1)} collective-permute-done((bf16[3,592,128]{2,1,0:T(8,128)(2,1)}, bf16[3,592,128]{2,1,0:T(8,128)(2,1)}, u32[]{:S(2)}, u32[]{:S(2)}) %collective-permute-start.6) | collective-permute-done | bytes 454688 | tf_op jit(solution)/shard_map/ppermute | solution.py:348
  57.7 1.0 copy-done.3
  58.7 1.0 copy-done.5
  59.7 19.8 %shard_map.110 = (f32[4,96,640]{2,1,0:T(8,128)S(1)}, bf16[4,96,640]{2,1,0:T(8,128)(2,1)S(1)}) custom-call(s32[24]{0:T(128)S(1)} %fusion.5.place_ref, s32[3]{0:T(128)S(1)} %pad_add_fusion.meta_ref, f32[1,768]{1,0:T(1,128)S(1)} %get-tuple-element.32.mean_a, f32[1,768]{1,0:T(1,128)S(1)} %get-tuple-element.33.istd_a, bf16[192,768]{1,0:T(8,128)(2,1)S(1)} %copy-done.5, ...), custom_call_target="tpu_custom_call" | custom-call | tf_op jit(solution)/shard_map/pallas_call | solution.py:298
  79.4 2.3 %collective-permute-start.7 = (bf16[4,96,640]{2,1,0:T(8,128)(2,1)S(1)}, bf16[4,96,640]{2,1,0:T(8,128)(2,1)S(1)}, u32[]{:S(2)}, u32[]{:S(2)}) collective-permute-start(bf16[4,96,640]{2,1,0:T(8,128)(2,1)S(1)} %get-tuple-element.38), channel_id=1, source_target_pairs={{0,1},{1,0},{2,3},{3,2},{4,5},{5,4},{6,7},{7,6},{8,9},{9,8},{10,11... | collective-permute-start | bytes 1474568 | tf_op jit(solution)/shard_map/ppermute | solution.py:348
  81.7 1.5 %collective-permute-done.7 = bf16[4,96,640]{2,1,0:T(8,128)(2,1)S(1)} collective-permute-done((bf16[4,96,640]{2,1,0:T(8,128)(2,1)S(1)}, bf16[4,96,640]{2,1,0:T(8,128)(2,1)S(1)}, u32[]{:S(2)}, u32[]{:S(2)}) %collective-permute-start.7) | collective-permute-done | bytes 491552 | tf_op jit(solution)/shard_map/ppermute | solution.py:348
  83.3 11.4 %all_to_all.20 = bf16[4,96,640]{2,1,0:T(8,128)(2,1)S(1)} all-to-all(bf16[4,96,640]{2,1,0:T(8,128)(2,1)S(1)} %add_convert_fusion), channel_id=1, replica_groups=mesh['y'=8,'zh'=2,'x'=4,'zt'=2,'zi'=3,'core'=2] {'x'}, dimensions={0} | all-to-all | bytes 983040 | tf_op jit(solution)/shard_map/all_to_all | solution.py:340
  94.9 14.9 %all_to_all.21 = bf16[8,12,640]{2,1,0:T(8,128)(2,1)S(1)} all-to-all(bf16[8,12,640]{2,1,0:T(8,128)(2,1)S(1)} %reshape.24), channel_id=1, replica_groups=mesh['y'=8,'zh'=2,'x'=4,'zt'=2,'zi'=3,'core'=2] {'y'}, dimensions={0} | all-to-all | bytes 245760 | tf_op jit(solution)/shard_map/all_to_all | solution.py:340
  109.9 21.0 %all_to_all.22 = bf16[12,6,640]{2,1,0:T(8,128)(2,1)S(1)} all-to-all(bf16[12,6,640]{2,1,0:T(8,128)(2,1)S(1)} %bitcast.38), channel_id=1, replica_groups=mesh['y'=8,'zh'=2,'x'=4,'zt'=2,'zi'=3,'core'=2] {'zh','zt','zi'}, dimensions={0} | all-to-all | bytes 184320 | tf_op jit(solution)/shard_map/all_to_all | solution.py:340
  130.9 6.1 %collective-permute-start.8 = (f32[6,640]{1,0:T(8,128)S(1)}, f32[6,640]{1,0:T(8,128)S(1)}, u32[]{:S(2)}, u32[]{:S(2)}) collective-permute-start(f32[6,640]{1,0:T(8,128)S(1)} %convert_reduce_fusion), channel_id=1, source_target_pairs={{0,1},{1,0},{2,3},{3,2},{4,5},{5,4},{6,7},{7,6},{8,9},{9,8},{10,11... | collective-permute-start | bytes 46088 | tf_op jit(solution)/shard_map/ppermute | solution.py:348
  137.1 0.8 collective-permute-done.8
  (43 shorter events, 2.0 us)
Async XLA Ops:
  0.0 20.4 %copy-start = (bf16[768,768]{1,0:T(8,128)(2,1)S(1)}, bf16[768,768]{1,0:T(8,128)(2,1)}, u32[]{:S(2)}) copy-start(bf16[768,768]{1,0:T(8,128)(2,1)} %param.20) | copy-start | bytes 3538948
  1.2 30.1 %collective-permute-start.1 = (bf16[592,128]{1,0:T(8,128)(2,1)S(1)}, bf16[592,128]{1,0:T(8,128)(2,1)S(1)}, u32[]{:S(2)}, u32[]{:S(2)}) collective-permute-start(bf16[592,128]{1,0:T(8,128)(2,1)S(1)} %get-tuple-element.40), channel_id=1, source_target_pairs={{0,2},{2,4},{4,0},{1,3},{3,5},{5,1},{6,8},{8,10},{10,6},{7,9},{9,1... | collective-permute-start | bytes 454664 | tf_op jit(solution)/shard_map/ppermute | solution.py:344
  6.0 25.3 %collective-permute-start.2 = (bf16[592,128]{1,0:T(8,128)(2,1)S(1)}, bf16[592,128]{1,0:T(8,128)(2,1)S(1)}, u32[]{:S(2)}, u32[]{:S(2)}) collective-permute-start(bf16[592,128]{1,0:T(8,128)(2,1)S(1)} %get-tuple-element.40), channel_id=1, source_target_pairs={{0,4},{2,0},{4,2},{1,5},{3,1},{5,3},{6,10},{8,6},{10,8},{7,11},{9,... | collective-permute-start | bytes 454664 | tf_op jit(solution)/shard_map/ppermute | solution.py:344
  9.8 21.7 %collective-permute-start = (bf16[592,128]{1,0:T(8,128)(2,1)S(1)}, bf16[592,128]{1,0:T(8,128)(2,1)}, u32[]{:S(2)}, u32[]{:S(2)}) collective-permute-start(bf16[592,128]{1,0:T(8,128)(2,1)S(1)} %get-tuple-element.40), channel_id=1, source_target_pairs={{0,6},{6,0},{1,7},{7,1},{2,8},{8,2},{3,9},{9,3},{4,10},{10,4},{5,1... | collective-permute-start | bytes 454664 | tf_op jit(solution)/shard_map/ppermute | solution.py:382
  21.8 34.3 %all-to-all-start = ((bf16[12,64,128]{2,1,0:T(8,128)(2,1)}), bf16[12,64,128]{2,1,0:T(8,128)(2,1)}, u32[]{:S(2)}, u32[]{:S(2)}) async-start(bf16[12,64,128]{2,1,0:T(8,128)(2,1)} %bitcast.15), calls=%async_computation | async-start | bytes 393216 | tf_op jit(solution)/shard_map/all_to_all | solution.py:340
  29.3 12.3 %copy-start.7 = (f32[768]{0:T(1024)S(1)}, f32[768]{0:T(1024)}, u32[]{:S(2)}) copy-start(f32[768]{0:T(1024)} %param.15) | copy-start | bytes 9220
  29.3 12.3 %copy-start.8 = (f32[768]{0:T(1024)S(1)}, f32[768]{0:T(1024)}, u32[]{:S(2)}) copy-start(f32[768]{0:T(1024)} %param.16) | copy-start | bytes 9220
  29.3 12.3 %copy-start.6 = (bf16[768,588]{0,1:T(8,128)(2,1)S(1)}, bf16[768,588]{0,1:T(8,128)(2,1)}, u32[]{:S(2)}) copy-start(bf16[768,588]{0,1:T(8,128)(2,1)} %param.14) | copy-start | bytes 2709508
  31.4 11.5 %copy-start.1 = (bf16[3,592,128]{2,1,0:T(8,128)(2,1)}, bf16[3,592,128]{2,1,0:T(8,128)(2,1)S(1)}, u32[]{:S(2)}) copy-start(bf16[3,592,128]{2,1,0:T(8,128)(2,1)S(1)} %pad_maximum_fusion.own_hbm.near_own_hbm) | copy-start | bytes 1363972
  31.4 15.0 %collective-permute-start.5 = (bf16[3,592,128]{2,1,0:T(8,128)(2,1)S(1)}, bf16[3,592,128]{2,1,0:T(8,128)(2,1)}, u32[]{:S(2)}, u32[]{:S(2)}) collective-permute-start(bf16[3,592,128]{2,1,0:T(8,128)(2,1)S(1)} %pad_maximum_fusion.own_hbm.near_own_hbm), channel_id=1, source_target_pairs={{0,1},{1,0},{2,3},{3,2},{4,5},{5,4},{6,7},{7,6},{8,9},{9,8},{10,11... | collective-permute-start | bytes 1363976 | tf_op jit(solution)/shard_map/ppermute | solution.py:348
  33.4 18.3 %collective-permute-start.4 = (bf16[592,128]{1,0:T(8,128)(2,1)}, bf16[592,128]{1,0:T(8,128)(2,1)}, u32[]{:S(2)}, u32[]{:S(2)}) collective-permute-start(bf16[592,128]{1,0:T(8,128)(2,1)} %collective-permute-done), channel_id=1, source_target_pairs={{0,4},{2,0},{4,2},{1,5},{3,1},{5,3},{6,10},{8,6},{10,8},{7,11},{9,... | collective-permute-start | bytes 454664 | tf_op jit(solution)/shard_map/ppermute | solution.py:344
  37.9 13.8 %collective-permute-start.3 = (bf16[592,128]{1,0:T(8,128)(2,1)}, bf16[592,128]{1,0:T(8,128)(2,1)}, u32[]{:S(2)}, u32[]{:S(2)}) collective-permute-start(bf16[592,128]{1,0:T(8,128)(2,1)} %collective-permute-done), channel_id=1, source_target_pairs={{0,2},{2,4},{4,0},{1,3},{3,5},{5,1},{6,8},{8,10},{10,6},{7,9},{9,1... | collective-permute-start | bytes 454664 | tf_op jit(solution)/shard_map/ppermute | solution.py:344
  46.7 1.0 copy-start.2
  47.7 8.3 %copy-start.9 = (s32[1,24]{1,0:T(1,128)S(1)}, s32[1,24]{1,0:T(1,128)}, u32[]{:S(2)}) copy-start(s32[1,24]{1,0:T(1,128)} %param.12) | copy-start | bytes 292
  51.0 0.7 copy-start.4
  53.6 4.1 %collective-permute-start.6 = (bf16[3,592,128]{2,1,0:T(8,128)(2,1)}, bf16[3,592,128]{2,1,0:T(8,128)(2,1)}, u32[]{:S(2)}, u32[]{:S(2)}) collective-permute-start(bf16[3,592,128]{2,1,0:T(8,128)(2,1)} %pad_maximum_fusion.1.far_own_hbm), channel_id=1, source_target_pairs={{0,1},{1,0},{2,3},{3,2},{4,5},{5,4},{6,7},{7,6},{8,9},{9,8},{10,11... | collective-permute-start | bytes 1363976 | tf_op jit(solution)/shard_map/ppermute | solution.py:348
  57.7 1.0 copy-start.3
  58.7 1.0 copy-start.5
  79.4 3.8 %collective-permute-start.7 = (bf16[4,96,640]{2,1,0:T(8,128)(2,1)S(1)}, bf16[4,96,640]{2,1,0:T(8,128)(2,1)S(1)}, u32[]{:S(2)}, u32[]{:S(2)}) collective-permute-start(bf16[4,96,640]{2,1,0:T(8,128)(2,1)S(1)} %get-tuple-element.38), channel_id=1, source_target_pairs={{0,1},{1,0},{2,3},{3,2},{4,5},{5,4},{6,7},{7,6},{8,9},{9,8},{10,11... | collective-permute-start | bytes 1474568 | tf_op jit(solution)/shard_map/ppermute | solution.py:348
  130.9 7.0 %collective-permute-start.8 = (f32[6,640]{1,0:T(8,128)S(1)}, f32[6,640]{1,0:T(8,128)S(1)}, u32[]{:S(2)}, u32[]{:S(2)}) collective-permute-start(f32[6,640]{1,0:T(8,128)S(1)} %convert_reduce_fusion), channel_id=1, source_target_pairs={{0,1},{1,0},{2,3},{3,2},{4,5},{5,4},{6,7},{7,6},{8,9},{9,8},{10,11... | collective-permute-start | bytes 46088 | tf_op jit(solution)/shard_map/ppermute | solution.py:348

commit v4 on v3

--- a/solution.py
+++ b/solution.py
@@ -23,6 +23,7 @@
 SCENE_VMEM = 38 << 20
 
 DP_AXES = ("y", "zh", "x")
+CHIP_AXES = ("zt", "zi")
 SEQ_AXES = ("zt", "zi", "core")
 
 
@@ -32,7 +33,6 @@
     )
 
 
-WQKV = slice(TOK_DEV, TOK_DEV + 3 * HEAD_DIM)
 FEATURES = [slice(r * 128, (r + 1) * 128) for r in range(D // 128)]
 KEYS = [slice(r * 128, (r + 1) * 128) for r in range(SEQ // 128)]
 
@@ -79,19 +79,49 @@
     return copies
 
 
+def unpack_weights(raw_ref, rows_ref, weight_ref, wqkv_ref, wqkv_t_ref, affine_ref):
+    weight_ref[...] = jnp.transpose(raw_ref[...])
+    for i in range(2):
+        affine_ref[i] = jnp.transpose(jnp.broadcast_to(rows_ref[i], (128, D)))
+    wqkv_t_ref[...] = jnp.transpose(wqkv_ref[...])
+
+
+def weight_scratch():
+    bf, f32 = jnp.bfloat16, jnp.float32
+    return [
+        pltpu.VMEM((PIX_PAD, D), bf),
+        pltpu.VMEM((2, 1, D), f32),
+        pltpu.VMEM((D, PIX_PAD), bf),
+        pltpu.VMEM((3 * HEAD_DIM, D), bf),
+        pltpu.VMEM((2, D, 128), f32),
+    ]
+
+
 def embed_kernel(
-    own_hbm, other_hbm, weight_hbm, pack_hbm, affine_hbm,
-    mean_ref, istd_ref, qkv_ref, pixel_ref, emb_ref, ln_ref,
-    own_ref, other_ref, weight_ref, pack_ref, affine_ref, sems, wqkv_t_ref,
+    meta_ref, own_hbm, other_hbm, raw_hbm, gain_hbm, bias_hbm, query_hbm, key_hbm, value_hbm,
+    mean_ref, istd_ref, qkv_ref, wqkv_ref,
+    raw_ref, rows_ref, weight_ref, wqkv_t_ref, affine_ref,
+    three_ref, pixel_ref, emb_ref, ln_ref, own_ref, other_ref, sems,
 ):
+    lanes = pl.ds(pl.multiple_of(meta_ref[3] * 128, 128), 128)
     loads = start_loads(
-        (own_hbm, other_hbm, weight_hbm, pack_hbm, affine_hbm),
-        (own_ref, other_ref, weight_ref, pack_ref, affine_ref),
+        (own_hbm, other_hbm, raw_hbm, gain_hbm, bias_hbm,
+         query_hbm.at[:, lanes], key_hbm.at[:, lanes], value_hbm.at[:, lanes]),
+        (own_ref, other_ref, raw_ref, rows_ref.at[0], rows_ref.at[1],
+         three_ref.at[0], three_ref.at[1], three_ref.at[2]),
         sems,
     )
     for load in loads:
         load.wait()
-    wqkv_t_ref[...] = jnp.transpose(pack_ref[:, WQKV])
+    for i in range(2):
+
+        @pl.when(meta_ref[2] == i)
+        def _():
+            for j in range(3):
+                half = three_ref[j, :, i * HEAD_DIM : (i + 1) * HEAD_DIM]
+                wqkv_ref[:, j * HEAD_DIM : (j + 1) * HEAD_DIM] = half
+
+    unpack_weights(raw_ref, rows_ref, weight_ref, wqkv_ref, wqkv_t_ref, affine_ref)
     join_blocks(own_ref, other_ref, pixel_ref)
     chunks = [slice(c * QB, (c + 1) * QB) for c in range(HALF // QB)]
     for c, at in enumerate(chunks):
@@ -103,7 +133,7 @@
         qkv_ref[:, at] = dot(wqkv_t_ref[...], ln_ref[c], 1, 0).astype(jnp.bfloat16)
 
 
-def embed_call(own, other, weight, affine, packed):
+def embed_call(meta, own, other, params, projections):
     bf, f32 = jnp.bfloat16, jnp.float32
     vmem = pl.BlockSpec(memory_space=pltpu.VMEM)
     return pl.pallas_call(
@@ -112,28 +142,33 @@
             jax.ShapeDtypeStruct((1, HALF), f32),
             jax.ShapeDtypeStruct((1, HALF), f32),
             jax.ShapeDtypeStruct((3 * HEAD_DIM, HALF), bf),
+            jax.ShapeDtypeStruct((D, 3 * HEAD_DIM), bf),
         ),
-        in_specs=[pl.BlockSpec(memory_space=pl.ANY)] * 5,
-        out_specs=(vmem,) * 3,
+        in_specs=[pl.BlockSpec(memory_space=pltpu.SMEM)]
+        + [pl.BlockSpec(memory_space=pl.ANY)] * 8,
+        out_specs=(vmem,) * 4,
         scratch_shapes=[
+            *weight_scratch(),
+            pltpu.VMEM((3, D, 128), bf),
             pltpu.VMEM((PIX_PAD, HALF), bf),
             pltpu.VMEM((HALF // QB, D, QB), f32),
             pltpu.VMEM((HALF // QB, D, QB), bf),
-            *(pltpu.VMEM(x.shape, x.dtype) for x in (own, other, weight, packed, affine)),
-            pltpu.SemaphoreType.DMA((5,)),
-            pltpu.VMEM((3 * HEAD_DIM, D), bf),
+            pltpu.VMEM(own.shape, bf),
+            pltpu.VMEM(other.shape, bf),
+            pltpu.SemaphoreType.DMA((8,)),
         ],
         compiler_params=pltpu.CompilerParams(vmem_limit_bytes=EMBED_VMEM),
-    )(own, other, weight, packed, affine)
+    )(meta, own, other, *params, *projections)
 
 
 def scene_kernel(
-    place_ref, meta_ref, mean_a, istd_a, qkv_a,
-    far_own_hbm, far_other_hbm, weight_hbm, pack_hbm, affine_hbm,
-    near_own_hbm, near_other_hbm, head_hbm,
+    place_ref, meta_ref, mean_a, istd_a, qkv_a, wqkv_ref,
+    far_own_hbm, far_other_hbm, near_own_hbm, near_other_hbm, head_hbm, cot_hbm,
+    raw_hbm, gain_hbm, bias_hbm,
     keep_ref, send_ref,
-    far_own, far_other, weight_ref, pack_ref, affine_ref,
-    near_own, near_other, head_ref, sems, wqkv_t_ref,
+    far_own, far_other, near_own, near_other, head_ref, cot_ref, sems,
+    raw_ref, rows_ref, weight_ref, wqkv_t_ref, affine_ref,
+    cot_t_ref,
     pix_a, pix_b, emb_ref, istd_b, qkv_b,
     k_ref, v_ref, kt_ref, qt_ref, q_ref, a_ref, live_ref, dqkv_ref, dk_ref, dv_ref, dt_ref,
     pick_ref, grad_ref, s_ref, dp_ref, p_ref, ds_ref, ln_ref, g_ref,
@@ -146,20 +181,21 @@
     steps = len(chunks)
 
     loads = start_loads(
-        (far_own_hbm, far_other_hbm, weight_hbm, pack_hbm, affine_hbm,
-         near_own_hbm, near_other_hbm, head_hbm),
-        (far_own, far_other, weight_ref, pack_ref, affine_ref,
-         near_own, near_other, head_ref),
+        (far_own_hbm, far_other_hbm, near_own_hbm, near_other_hbm, head_hbm, cot_hbm,
+         raw_hbm, gain_hbm, bias_hbm),
+        (far_own, far_other, near_own, near_other, head_ref, cot_ref,
+         raw_ref, rows_ref.at[0], rows_ref.at[1]),
         sems,
     )
-    for load in loads[:3]:
+    for load in loads:
         load.wait()
+    unpack_weights(raw_ref, rows_ref, weight_ref, wqkv_ref, wqkv_t_ref, affine_ref)
+    token = position * TOK_DEV + lax.broadcasted_iota(jnp.int32, (TOK_DEV, D), 0)
+    cot_live = jnp.where(token < valid * TILE_TOK, cot_ref[...].astype(f32), 0.0)
+    cot_t_ref[...] = jnp.transpose(cot_live).astype(bf)
     join_blocks(far_own, far_other, pix_b)
     for c, at in enumerate(half_chunks):
         emb_ref[c] = dot(weight_ref[...], pix_b[:, at], 1, 0)
-    for load in loads[3:]:
-        load.wait()
-    wqkv_t_ref[...] = jnp.transpose(pack_ref[:, WQKV])
     join_blocks(near_own, near_other, pix_a)
     for b in range(HEADS):
         rows = jnp.transpose(head_ref[b])
@@ -231,7 +267,7 @@
 
     def norm_grad(c, normed_ref, inv_std):
         slot = c % 2
-        g_ref[slot] = dot(pack_ref[:, WQKV], dqkv_ref[:, chunks[c]], 1, 0)
+        g_ref[slot] = dot(wqkv_ref[...], dqkv_ref[:, chunks[c]], 1, 0)
         first = jnp.zeros((8, QB), f32)
         second = jnp.zeros((8, QB), f32)
         for rows in FEATURES:
@@ -278,7 +314,7 @@
             fill(pix_b)
 
     grad_ref[...] += dot(dt_ref[:, :HALF], pix_a[...], 1, 1) + dot(
-        pack_ref[:, :TOK_DEV], pick_ref[...].astype(bf), 1, 1
+        cot_t_ref[...], pick_ref[...].astype(bf), 1, 1
     )
     first_core = core == 0
     for y in range(8):
@@ -290,23 +326,24 @@
                 send_ref[x, spot : spot + 6, :] = jnp.where(first_core, high, low).astype(bf)
 
 
-def scene_call(place, meta, near, far, front, head_t, weight, packed, affine):
+def scene_call(place, meta, near, far, front, head_t, cot, params):
     bf, f32 = jnp.bfloat16, jnp.float32
     smem = pl.BlockSpec(memory_space=pltpu.SMEM)
     vmem = pl.BlockSpec(memory_space=pltpu.VMEM)
-    loaded = (*far, weight, packed, affine, *near, head_t)
+    loaded = (*far, *near, head_t, cot)
     return pl.pallas_call(
         scene_kernel,
         out_shape=(
             jax.ShapeDtypeStruct((4, 96, PIX_PAD), f32),
             jax.ShapeDtypeStruct((4, 96, PIX_PAD), bf),
         ),
-        in_specs=[smem, smem] + [vmem] * 3 + [pl.BlockSpec(memory_space=pl.ANY)] * 8,
+        in_specs=[smem, smem] + [vmem] * 4 + [pl.BlockSpec(memory_space=pl.ANY)] * 9,
         out_specs=(vmem, vmem),
         scratch_shapes=[
             *(pltpu.VMEM(x.shape, x.dtype) for x in loaded),
-            pltpu.SemaphoreType.DMA((8,)),
-            pltpu.VMEM((3 * HEAD_DIM, D), bf),
+            pltpu.SemaphoreType.DMA((9,)),
+            *weight_scratch(),
+            pltpu.VMEM((D, TOK_DEV), bf),
             pltpu.VMEM((PIX_PAD, HALF), bf),
             pltpu.VMEM((PIX_PAD, HALF), bf),
             pltpu.VMEM((HALF // QB, D, QB), f32),
@@ -333,7 +370,7 @@
             pltpu.VMEM((2, D, QB), f32),
         ],
         compiler_params=pltpu.CompilerParams(vmem_limit_bytes=SCENE_VMEM),
-    )(place, meta, *front, *loaded)
+    )(place, meta, *front, *loaded, *params)
 
 
 def exchange(x, axes):
@@ -386,27 +423,21 @@
     cot_rows = cotangent[0]
     cot_live = jnp.where(live_rows[:, None], cot_rows, jnp.zeros_like(cot_rows))
     d_attn_t = dot(w_out, cot_live, 1, 1).astype(bf).reshape(HEADS, HEAD_DIM, TOK_DEV)
-    start = position * HEAD_DIM
-    parts = [lax.dynamic_slice_in_dim(w, start, HEAD_DIM, 1) for w in (w_query, w_key, w_value)]
-    packed = jnp.concatenate([cot_live.T, *parts, jnp.zeros((D, HEAD_DIM), bf)], axis=1)
-    weight = jnp.pad(patch_weight, ((0, 0), (0, PIX_PAD - PIX)))
-    affine = jnp.broadcast_to(jnp.stack([norm_gain, norm_bias])[:, :, None], (2, D, 128))
-    place = place_of(tile_list[0], zt, lax.axis_index("zi"), core)
-    meta = jnp.stack([valid_tiles[0], position, core])
-
     head_t = exchange(d_attn_t, SEQ_AXES)
     near_own = jnp.stack([pixels, *near_shifts])
     across, near_own = lax.optimization_barrier((across, near_own))
     shifted = shift_chips(across)
     near = (near_own, swap_core(near_own))
-    packed, weight, affine, near = lax.optimization_barrier((packed, weight, affine, near))
-    front = embed_call(*near, weight, affine, packed)
+
+    raw = jnp.pad(patch_weight.T, ((0, PIX_PAD - PIX), (0, 0)))
+    params = (raw, norm_gain[None], norm_bias[None])
+    place = place_of(tile_list[0], zt, lax.axis_index("zi"), core)
+    meta = jnp.stack([valid_tiles[0], position, core, lax.axis_index(CHIP_AXES)])
+    front = embed_call(meta, *near, params, (w_query, w_key, w_value))
     shifted, front = lax.optimization_barrier((shifted, front))
     far_own = jnp.stack([across, *shifted])
     far = (far_own, swap_core(far_own))
-    keep, send = scene_call(
-        place, meta, near, far, front, head_t, weight, packed, affine
-    )
+    keep, send = scene_call(place, meta, near, far, front, head_t, cot_rows, params)
 
     got = swap_core(send)
     mine = (keep + got.astype(f32)).astype(bf)

time: 139 us -> 144 us (1.036)
  starting transfers between devices: 44 us -> 52.2 us
  local copies, waits for them, and re-layouts: 15.7 us -> 11.5 us
  waiting for transfers between devices: 3.93 us -> 7.4 us
  blocking collectives: 47.4 us -> 44.9 us
    ppermute x4, starting transfers between devices: 12.7 us -> 20.5 us  [swap_core(): return lax.ppermute(x, 'core', [(0, 1), (1, 0)])]
    dynamic_slice x2 -> x0, local copies, waits for them, and re-layouts: 3.78 us -> none  [per_device(): lax.dynamic_slice_in_dim(w, start, HEAD_DIM, 1)]
    ppermute x1, waiting for transfers between devices: 0.01 us -> 3.01 us  [per_device(): across = lax.ppermute(pixels, 'zt', [(0, 1), (1, 0)])]
    all_to_all x3, blocking collectives: 47.4 us -> 44.9 us  [exchange(): return lax.all_to_all(x, axes, 0, 0, tiled=True)]
    unnamed x22 -> x26, local copies, waits for them, and re-layouts: 6.14 us -> 8.18 us
    all_to_all x1, starting transfers between devices: 7.51 us -> 9.12 us  [exchange(): return lax.all_to_all(x, axes, 0, 0, tiled=True)]
  transfers between devices with their start and end apart: 10 -> 10, of which waited for: 3 -> 4; matrix products, arithmetic and copies ran while one was open for 10% -> 3% of each run, Pallas kernels for 2% -> 3%
where the time goes in v4:
time: 144 us; the launch traced here: 143 us
  starting transfers between devices  52.2 us (36%)
  blocking collectives  44.9 us (31%)
  Pallas kernels  23.1 us (16%)
  local copies, waits for them, and re-layouts  11.5 us (8%)
  waiting for transfers between devices  7.4 us (5%)
  other arithmetic  2.2 us (2%)
    all_to_all x3, blocking collectives, exchange(): return lax.all_to_all(x, axes, 0, 0, tiled=True)  44.9 us
    ppermute x4, starting transfers between devices, swap_core(): return lax.ppermute(x, 'core', [(0, 1), (1, 0)])  20.5 us
    pallas_call x1, Pallas kernels, scene_call(): pl.pallas_call(scene_kernel, out_shape=(jax.ShapeDtypeStruct((4, 96, PIX_...  19.2 us
    ppermute x4, starting transfers between devices, shift_chips(): lax.ppermute(x, 'zi', [(i, (i + hop) % 3) for i in range(3)])  13.8 us
    all_to_all x1, starting transfers between devices, exchange(): return lax.all_to_all(x, axes, 0, 0, tiled=True)  9.12 us
    ppermute x1, starting transfers between devices, per_device(): across = lax.ppermute(pixels, 'zt', [(0, 1), (1, 0)])  8.83 us
    unnamed x26, local copies, waits for them, and re-layouts  8.18 us
    ppermute x4, waiting for transfers between devices, swap_core(): return lax.ppermute(x, 'core', [(0, 1), (1, 0)])  4.37 us
  transfers between devices with their start and end apart: 10, of which 4 were waited for; matrix products, arithmetic and copies ran while one was open for 3% of the time, Pallas kernels for 3%

profile of v4, /device:TPU:1, one launch (start us, length us, event | category | flops | bytes accessed | tf_op | source)
XLA Modules:
  0.0 142.8 jit_solution(9367766354336402579)
XLA Ops:
  0.0 1.2 copy.16
  1.2 4.8 %collective-permute-start.1 = (bf16[592,128]{1,0:T(8,128)(2,1)S(1)}, bf16[592,128]{1,0:T(8,128)(2,1)S(1)}, u32[]{:S(2)}, u32[]{:S(2)}) collective-permute-start(bf16[592,128]{1,0:T(8,128)(2,1)S(1)} %get-tuple-element.34), channel_id=1, source_target_pairs={{0,2},{2,4},{4,0},{1,3},{3,5},{5,1},{6,8},{8,10},{10,6},{7,9},{9,1... | collective-permute-start | bytes 454664 | tf_op jit(solution)/shard_map/ppermute | solution.py:381
  6.0 3.7 %collective-permute-start.2 = (bf16[592,128]{1,0:T(8,128)(2,1)S(1)}, bf16[592,128]{1,0:T(8,128)(2,1)S(1)}, u32[]{:S(2)}, u32[]{:S(2)}) collective-permute-start(bf16[592,128]{1,0:T(8,128)(2,1)S(1)} %get-tuple-element.34), channel_id=1, source_target_pairs={{0,4},{2,0},{4,2},{1,5},{3,1},{5,3},{6,10},{8,6},{10,8},{7,11},{9,... | collective-permute-start | bytes 454664 | tf_op jit(solution)/shard_map/ppermute | solution.py:381
  9.8 8.8 %collective-permute-start = (bf16[592,128]{1,0:T(8,128)(2,1)S(1)}, bf16[592,128]{1,0:T(8,128)(2,1)}, u32[]{:S(2)}, u32[]{:S(2)}) collective-permute-start(bf16[592,128]{1,0:T(8,128)(2,1)S(1)} %get-tuple-element.34), channel_id=1, source_target_pairs={{0,6},{6,0},{1,7},{7,1},{2,8},{8,2},{3,9},{9,3},{4,10},{10,4},{5,1... | collective-permute-start | bytes 454664 | tf_op jit(solution)/shard_map/ppermute | solution.py:419
  19.4 3.0 %collective-permute-done = bf16[592,128]{1,0:T(8,128)(2,1)} collective-permute-done((bf16[592,128]{1,0:T(8,128)(2,1)S(1)}, bf16[592,128]{1,0:T(8,128)(2,1)}, u32[]{:S(2)}, u32[]{:S(2)}) %collective-permute-start) | collective-permute-done | bytes 151584 | tf_op jit(solution)/shard_map/ppermute | solution.py:419
  22.4 10.4 %collective-permute-start.5 = (bf16[3,592,128]{2,1,0:T(8,128)(2,1)S(1)}, bf16[3,592,128]{2,1,0:T(8,128)(2,1)S(1)}, u32[]{:S(2)}, u32[]{:S(2)}) collective-permute-start(bf16[3,592,128]{2,1,0:T(8,128)(2,1)S(1)} %pad_maximum_fusion.own_hbm.near_own_hbm), channel_id=1, source_target_pairs={{0,1},{1,0},{2,3},{3,2},{4,5},{5,4},{6,7},{7,6},{8,9},{9,8},{10,11... | collective-permute-start | bytes 1363976 | tf_op jit(solution)/shard_map/ppermute | solution.py:385
  32.8 1.9 %collective-permute-start.4 = (bf16[592,128]{1,0:T(8,128)(2,1)}, bf16[592,128]{1,0:T(8,128)(2,1)}, u32[]{:S(2)}, u32[]{:S(2)}) collective-permute-start(bf16[592,128]{1,0:T(8,128)(2,1)} %collective-permute-done), channel_id=1, source_target_pairs={{0,4},{2,0},{4,2},{1,5},{3,1},{5,3},{6,10},{8,6},{10,8},{7,11},{9,... | collective-permute-start | bytes 454664 | tf_op jit(solution)/shard_map/ppermute | solution.py:381
  34.7 3.4 %collective-permute-start.3 = (bf16[592,128]{1,0:T(8,128)(2,1)}, bf16[592,128]{1,0:T(8,128)(2,1)}, u32[]{:S(2)}, u32[]{:S(2)}) collective-permute-start(bf16[592,128]{1,0:T(8,128)(2,1)} %collective-permute-done), channel_id=1, source_target_pairs={{0,2},{2,4},{4,0},{1,3},{3,5},{5,1},{6,8},{8,10},{10,6},{7,9},{9,1... | collective-permute-start | bytes 454664 | tf_op jit(solution)/shard_map/ppermute | solution.py:381
  38.7 0.8 copy.17
  39.5 9.1 %all-to-all-start = ((bf16[12,64,128]{2,1,0:T(8,128)(2,1)}), bf16[12,64,128]{2,1,0:T(8,128)(2,1)}, u32[]{:S(2)}, u32[]{:S(2)}) async-start(bf16[12,64,128]{2,1,0:T(8,128)(2,1)} %bitcast.16), calls=%async_computation | async-start | bytes 393216 | tf_op jit(solution)/shard_map/all_to_all | solution.py:377
  48.6 1.2 pad.9.raw_hbm
  50.0 1.3 copy-done.1
  51.2 1.3 copy-done.2
  52.5 1.3 copy-done.3
  53.8 3.9 %shard_map.109 = (f32[1,768]{1,0:T(1,128)S(1)}, f32[1,768]{1,0:T(1,128)S(1)}, bf16[192,768]{1,0:T(8,128)(2,1)S(1)}, bf16[768,192]{1,0:T(8,128)(2,1)S(1)}) custom-call(s32[4]{0:T(128)S(1)} %pad_add_fusion.meta_ref, bf16[3,592,128]{2,1,0:T(8,128)(2,1)S(1)} %pad_maximum_fusion.own_hbm.near_own_hbm, ...), custom_call_target="tpu_custom_call" | custom-call | tf_op jit(solution)/shard_map/pallas_call | solution.py:139
  57.7 0.7 copy-done.6
  58.4 0.7 copy-done.8
  59.1 1.1 pad_maximum_fusion.1.far_own_hbm
  60.2 1.9 %collective-permute-start.6 = (bf16[3,592,128]{2,1,0:T(8,128)(2,1)S(1)}, bf16[3,592,128]{2,1,0:T(8,128)(2,1)}, u32[]{:S(2)}, u32[]{:S(2)}) collective-permute-start(bf16[3,592,128]{2,1,0:T(8,128)(2,1)S(1)} %pad_maximum_fusion.1.far_own_hbm), channel_id=1, source_target_pairs={{0,1},{1,0},{2,3},{3,2},{4,5},{5,4},{6,7},{7,6},{8,9},{9,8},{10,11... | collective-permute-start | bytes 1363976 | tf_op jit(solution)/shard_map/ppermute | solution.py:385
  62.2 1.8 %collective-permute-done.6.far_other_hbm = bf16[3,592,128]{2,1,0:T(8,128)(2,1)} collective-permute-done((bf16[3,592,128]{2,1,0:T(8,128)(2,1)S(1)}, bf16[3,592,128]{2,1,0:T(8,128)(2,1)}, u32[]{:S(2)}, u32[]{:S(2)}) %collective-permute-start.6) | collective-permute-done | bytes 454688 | tf_op jit(solution)/shard_map/ppermute | solution.py:385
  64.1 0.9 copy-done.5
  65.0 1.0 copy-done.7
  66.0 1.0 copy-done.9
  67.0 19.2 %shard_map.110 = (f32[4,96,640]{2,1,0:T(8,128)S(1)}, bf16[4,96,640]{2,1,0:T(8,128)(2,1)S(1)}) custom-call(s32[24]{0:T(128)S(1)} %fusion.6.place_ref, s32[4]{0:T(128)S(1)} %pad_add_fusion.meta_ref, f32[1,768]{1,0:T(1,128)S(1)} %get-tuple-element.25.mean_a, f32[1,768]{1,0:T(1,128)S(1)} %get-tuple-element.26.istd_a, bf16[192,768]{1,0:T(8,128)(2,1)S(1)} %copy-done.9, ...), custom_call_target="tpu_custom_call" | custom-call | tf_op jit(solution)/shard_map/pallas_call | solution.py:334
  86.2 2.0 %collective-permute-start.7 = (bf16[4,96,640]{2,1,0:T(8,128)(2,1)S(1)}, bf16[4,96,640]{2,1,0:T(8,128)(2,1)S(1)}, u32[]{:S(2)}, u32[]{:S(2)}) collective-permute-start(bf16[4,96,640]{2,1,0:T(8,128)(2,1)S(1)} %get-tuple-element.32), channel_id=1, source_target_pairs={{0,1},{1,0},{2,3},{3,2},{4,5},{5,4},{6,7},{7,6},{8,9},{9,8},{10,11... | collective-permute-start | bytes 1474568 | tf_op jit(solution)/shard_map/ppermute | solution.py:385
  88.2 1.7 %collective-permute-done.7 = bf16[4,96,640]{2,1,0:T(8,128)(2,1)S(1)} collective-permute-done((bf16[4,96,640]{2,1,0:T(8,128)(2,1)S(1)}, bf16[4,96,640]{2,1,0:T(8,128)(2,1)S(1)}, u32[]{:S(2)}, u32[]{:S(2)}) %collective-permute-start.7) | collective-permute-done | bytes 491552 | tf_op jit(solution)/shard_map/ppermute | solution.py:385
  90.1 12.3 %all_to_all.20 = bf16[4,96,640]{2,1,0:T(8,128)(2,1)S(1)} all-to-all(bf16[4,96,640]{2,1,0:T(8,128)(2,1)S(1)} %add_convert_fusion), channel_id=1, replica_groups=mesh['y'=8,'zh'=2,'x'=4,'zt'=2,'zi'=3,'core'=2] {'x'}, dimensions={0} | all-to-all | bytes 983040 | tf_op jit(solution)/shard_map/all_to_all | solution.py:377
  102.5 14.9 %all_to_all.21 = bf16[8,12,640]{2,1,0:T(8,128)(2,1)S(1)} all-to-all(bf16[8,12,640]{2,1,0:T(8,128)(2,1)S(1)} %reshape.23), channel_id=1, replica_groups=mesh['y'=8,'zh'=2,'x'=4,'zt'=2,'zi'=3,'core'=2] {'y'}, dimensions={0} | all-to-all | bytes 245760 | tf_op jit(solution)/shard_map/all_to_all | solution.py:377
  117.5 17.7 %all_to_all.22 = bf16[12,6,640]{2,1,0:T(8,128)(2,1)S(1)} all-to-all(bf16[12,6,640]{2,1,0:T(8,128)(2,1)S(1)} %bitcast.40), channel_id=1, replica_groups=mesh['y'=8,'zh'=2,'x'=4,'zt'=2,'zi'=3,'core'=2] {'zh','zt','zi'}, dimensions={0} | all-to-all | bytes 184320 | tf_op jit(solution)/shard_map/all_to_all | solution.py:377
  135.2 6.1 %collective-permute-start.8 = (f32[6,640]{1,0:T(8,128)S(1)}, f32[6,640]{1,0:T(8,128)S(1)}, u32[]{:S(2)}, u32[]{:S(2)}) collective-permute-start(f32[6,640]{1,0:T(8,128)S(1)} %convert_reduce_fusion), channel_id=1, source_target_pairs={{0,1},{1,0},{2,3},{3,2},{4,5},{5,4},{6,7},{7,6},{8,9},{9,8},{10,11... | collective-permute-start | bytes 46088 | tf_op jit(solution)/shard_map/ppermute | solution.py:385
  141.3 0.8 collective-permute-done.8
  142.2 0.6 fusion.4
  (40 shorter events, 1.2 us)
Async XLA Ops:
  0.0 38.1 %copy-start = (bf16[768,768]{1,0:T(8,128)(2,1)S(1)}, bf16[768,768]{1,0:T(8,128)(2,1)}, u32[]{:S(2)}) copy-start(bf16[768,768]{1,0:T(8,128)(2,1)} %param.20) | copy-start | bytes 3538948
  0.0 38.1 %copy-start.4 = (bf16[1,128,768]{2,1,0:T(8,128)(2,1)S(1)}, bf16[1,128,768]{2,1,0:T(8,128)(2,1)}, u32[]{:S(2)}) copy-start(bf16[1,128,768]{2,1,0:T(8,128)(2,1)} %param.21) | copy-start | bytes 589828
  1.2 18.1 %collective-permute-start.1 = (bf16[592,128]{1,0:T(8,128)(2,1)S(1)}, bf16[592,128]{1,0:T(8,128)(2,1)S(1)}, u32[]{:S(2)}, u32[]{:S(2)}) collective-permute-start(bf16[592,128]{1,0:T(8,128)(2,1)S(1)} %get-tuple-element.34), channel_id=1, source_target_pairs={{0,2},{2,4},{4,0},{1,3},{3,5},{5,1},{6,8},{8,10},{10,6},{7,9},{9,1... | collective-permute-start | bytes 454664 | tf_op jit(solution)/shard_map/ppermute | solution.py:381
  6.0 13.3 %collective-permute-start.2 = (bf16[592,128]{1,0:T(8,128)(2,1)S(1)}, bf16[592,128]{1,0:T(8,128)(2,1)S(1)}, u32[]{:S(2)}, u32[]{:S(2)}) collective-permute-start(bf16[592,128]{1,0:T(8,128)(2,1)S(1)} %get-tuple-element.34), channel_id=1, source_target_pairs={{0,4},{2,0},{4,2},{1,5},{3,1},{5,3},{6,10},{8,6},{10,8},{7,11},{9,... | collective-permute-start | bytes 454664 | tf_op jit(solution)/shard_map/ppermute | solution.py:381
  9.8 12.6 %collective-permute-start = (bf16[592,128]{1,0:T(8,128)(2,1)S(1)}, bf16[592,128]{1,0:T(8,128)(2,1)}, u32[]{:S(2)}, u32[]{:S(2)}) collective-permute-start(bf16[592,128]{1,0:T(8,128)(2,1)S(1)} %get-tuple-element.34), channel_id=1, source_target_pairs={{0,6},{6,0},{1,7},{7,1},{2,8},{8,2},{3,9},{9,3},{4,10},{10,4},{5,1... | collective-permute-start | bytes 454664 | tf_op jit(solution)/shard_map/ppermute | solution.py:419
  22.4 27.6 %collective-permute-start.5 = (bf16[3,592,128]{2,1,0:T(8,128)(2,1)S(1)}, bf16[3,592,128]{2,1,0:T(8,128)(2,1)S(1)}, u32[]{:S(2)}, u32[]{:S(2)}) collective-permute-start(bf16[3,592,128]{2,1,0:T(8,128)(2,1)S(1)} %pad_maximum_fusion.own_hbm.near_own_hbm), channel_id=1, source_target_pairs={{0,1},{1,0},{2,3},{3,2},{4,5},{5,4},{6,7},{7,6},{8,9},{9,8},{10,11... | collective-permute-start | bytes 1363976 | tf_op jit(solution)/shard_map/ppermute | solution.py:385
  32.8 15.8 %copy-start.10 = (f32[768]{0:T(1024)S(1)}, f32[768]{0:T(1024)}, u32[]{:S(2)}) copy-start(f32[768]{0:T(1024)} %param.15) | copy-start | bytes 9220
  32.8 15.8 %copy-start.11 = (f32[768]{0:T(1024)S(1)}, f32[768]{0:T(1024)}, u32[]{:S(2)}) copy-start(f32[768]{0:T(1024)} %param.16) | copy-start | bytes 9220
  32.8 26.3 %collective-permute-start.4 = (bf16[592,128]{1,0:T(8,128)(2,1)}, bf16[592,128]{1,0:T(8,128)(2,1)}, u32[]{:S(2)}, u32[]{:S(2)}) collective-permute-start(bf16[592,128]{1,0:T(8,128)(2,1)} %collective-permute-done), channel_id=1, source_target_pairs={{0,4},{2,0},{4,2},{1,5},{3,1},{5,3},{6,10},{8,6},{10,8},{7,11},{9,... | collective-permute-start | bytes 454664 | tf_op jit(solution)/shard_map/ppermute | solution.py:381
  34.7 24.4 %collective-permute-start.3 = (bf16[592,128]{1,0:T(8,128)(2,1)}, bf16[592,128]{1,0:T(8,128)(2,1)}, u32[]{:S(2)}, u32[]{:S(2)}) collective-permute-start(bf16[592,128]{1,0:T(8,128)(2,1)} %collective-permute-done), channel_id=1, source_target_pairs={{0,2},{2,4},{4,0},{1,3},{3,5},{5,1},{6,8},{8,10},{10,6},{7,9},{9,1... | collective-permute-start | bytes 454664 | tf_op jit(solution)/shard_map/ppermute | solution.py:381
  39.5 22.8 %all-to-all-start = ((bf16[12,64,128]{2,1,0:T(8,128)(2,1)}), bf16[12,64,128]{2,1,0:T(8,128)(2,1)}, u32[]{:S(2)}, u32[]{:S(2)}) async-start(bf16[12,64,128]{2,1,0:T(8,128)(2,1)} %bitcast.16), calls=%async_computation | async-start | bytes 393216 | tf_op jit(solution)/shard_map/all_to_all | solution.py:377
  50.0 1.3 copy-start.1
  51.2 1.3 copy-start.2
  52.5 1.3 copy-start.3
  53.8 8.4 %copy-start.12 = (s32[1,24]{1,0:T(1,128)S(1)}, s32[1,24]{1,0:T(1,128)}, u32[]{:S(2)}) copy-start(s32[1,24]{1,0:T(1,128)} %param.12) | copy-start | bytes 292
  57.7 0.7 copy-start.6
  58.4 0.7 copy-start.8
  60.2 3.8 %collective-permute-start.6 = (bf16[3,592,128]{2,1,0:T(8,128)(2,1)S(1)}, bf16[3,592,128]{2,1,0:T(8,128)(2,1)}, u32[]{:S(2)}, u32[]{:S(2)}) collective-permute-start(bf16[3,592,128]{2,1,0:T(8,128)(2,1)S(1)} %pad_maximum_fusion.1.far_own_hbm), channel_id=1, source_target_pairs={{0,1},{1,0},{2,3},{3,2},{4,5},{5,4},{6,7},{7,6},{8,9},{9,8},{10,11... | collective-permute-start | bytes 1363976 | tf_op jit(solution)/shard_map/ppermute | solution.py:385
  64.1 0.9 copy-start.5
  65.0 1.0 copy-start.7
  66.0 1.0 copy-start.9
  86.2 3.8 %collective-permute-start.7 = (bf16[4,96,640]{2,1,0:T(8,128)(2,1)S(1)}, bf16[4,96,640]{2,1,0:T(8,128)(2,1)S(1)}, u32[]{:S(2)}, u32[]{:S(2)}) collective-permute-start(bf16[4,96,640]{2,1,0:T(8,128)(2,1)S(1)} %get-tuple-element.32), channel_id=1, source_target_pairs={{0,1},{1,0},{2,3},{3,2},{4,5},{5,4},{6,7},{7,6},{8,9},{9,8},{10,11... | collective-permute-start | bytes 1474568 | tf_op jit(solution)/shard_map/ppermute | solution.py:385
  135.2 7.0 %collective-permute-start.8 = (f32[6,640]{1,0:T(8,128)S(1)}, f32[6,640]{1,0:T(8,128)S(1)}, u32[]{:S(2)}, u32[]{:S(2)}) collective-permute-start(f32[6,640]{1,0:T(8,128)S(1)} %convert_reduce_fusion), channel_id=1, source_target_pairs={{0,1},{1,0},{2,3},{3,2},{4,5},{5,4},{6,7},{7,6},{8,9},{9,8},{10,11... | collective-permute-start | bytes 46088 | tf_op jit(solution)/shard_map/ppermute | solution.py:385
